TPU v7x, 32 devices: a whole 2x2x4 slice. The times are simulated.
32 devices in a mesh: wide: 4 (over y, core), sixteen: 8 (over z, x).
Axes of the slice: x: 2, y: 2, z: 4, core: 2. Of those that a mesh axis runs over, the one named last changes fastest.
Arguments:
- observations: float32 [64, 256, 512], P(None, 'sixteen', 'wide'), may hold values from -60 to 60
- huber_scale: float32 [64], replicated, may hold values from 0.5 to 2
- observed: int32 [256, 512], P('sixteen', 'wide'), may hold values from 0 to 1, as said below
- jitter: float32 [2, 256, 512], P(None, 'sixteen', 'wide'), may hold values from -0.4 to 0.4
- owner_map: int32 [4, 64], P('wide'), may hold values from 0 to 7, as said below
- neighbours: int32 [4, 64, 6], P('wide'), may hold values from 0 to 63, as said below
Outputs:
- solution: float32 [4, 8, 64, 8, 512], P('wide', 'sixteen')
- residual: float32 [4, 8, 64, 8, 512], P('wide', 'sixteen')
Inputs may be any that keep to these rules, and one draw needn't show every extreme that they name: At least one whole lattice row and at least one whole lattice column hold no observed point. `owner_map`: in each column group every device along sixteen holds 8 blocks (block g on device g // 8) and sends them to 8 different owners; every owner receives exactly 8 blocks, each from a different device. `neighbours`: block g of a column group lists g + d and g - d modulo 64 for each of half of 6 different offsets d between 1 and 4; all blocks of one group use the same offsets, so every list holds 6 different blocks and the relation is symmetric.
All inputs are finite; a program needn't handle non-finite values.
Results may differ from a plain program's by a relative error of at most 0.0003.
Values sent between devices are 32-bit elements; how exact they have to be, the bound alone decides.
A program may use at most 192 MiB of HBM per device.

v0:
```python
import jax
import jax.numpy as jnp
from jax import lax
from jax.sharding import PartitionSpec as P

BLOCK = 512
BLOCKS_DEV = 8
REACH = 4
NEIGHBOURS = 6
SWEEPS = 2
ITERS = 2


HUBER_EDGE = 1.345
NUGGET_TERM = 1.0
SILL_TERM = 0.02
ROOT_THREE = 1.7320508075688772
EXACT = lax.Precision.HIGHEST


def padded(shard, sides, width):
    for axis, dim in sides:
        peers, length = (lax.axis_size(axis), shard.shape[dim])
        up = [(i, (i + 1) % peers) for i in range(peers)]
        down = [(j, i) for i, j in up]
        last = lax.slice_in_dim(shard, length - width, length, axis=dim)
        initial = lax.slice_in_dim(shard, 0, width, axis=dim)
        before = lax.ppermute(last, axis, up)
        after = lax.ppermute(initial, axis, down)
        shard = jnp.concatenate([before, shard, after], axis=dim)
    return shard


def covariance(centre, others, strip_rows):
    spread = 2.0 * strip_rows
    cutoff = 6.0 * strip_rows
    row_gap = others[0][:, :, None] - centre[0][None, None, :]
    col_gap = others[1][:, :, None] - centre[1][None, None, :]
    distance = jnp.sqrt(row_gap * row_gap + col_gap * col_gap)
    scaled = ROOT_THREE * distance / spread
    fading = jnp.maximum(1.0 - distance / cutoff, 0.0)
    return (
        SILL_TERM * (1.0 + scaled) * jnp.exp(-scaled) * fading**4 * (1.0 + 4.0 * distance / cutoff)
    )


def owned_table(group_map, owners, per_owner):
    total_strips = group_map.shape[0]
    member = (group_map[None, :] == jnp.arange(owners, dtype=jnp.int32)[:, None]).astype(jnp.int32)
    ranked = jnp.cumsum(member, axis=1, dtype=jnp.int32) - 1
    slot_hit = (ranked[:, :, None] == jnp.arange(per_owner, dtype=jnp.int32)[None, None, :]).astype(
        jnp.int32
    ) * member[:, :, None]
    numbers = jnp.arange(total_strips, dtype=jnp.int32)
    return jnp.sum(slot_hit * numbers[None, :, None], axis=1, dtype=jnp.int32)


def outgoing(observed_values, targets, owners):
    chooser = (targets[:, None] == jnp.arange(owners, dtype=jnp.int32)[None, :]).astype(jnp.float32)
    return jnp.einsum("ckb,ko->cob", observed_values, chooser, precision=EXACT)


def incoming(observed_values, owned_ids, per_owner):
    sources = observed_values.shape[1]
    chooser = (
        owned_ids[:, None] // per_owner == jnp.arange(sources, dtype=jnp.int32)[None, :]
    ).astype(jnp.float32)
    return jnp.einsum("csb,js->cjb", observed_values, chooser, precision=EXACT)


def sum_rows(observed_values):
    return lax.psum(observed_values, "wide")


def sum_columns(observed_values):
    return lax.psum(observed_values, "sixteen")


def on_device(observations, huber_scale, observed, jitter, owner_map, neighbours):
    fields, row_dev, col_dev = observations.shape
    sixteen_size = lax.axis_size("sixteen")
    my_place = lax.axis_index("sixteen")
    group_place = lax.axis_index("wide")
    strip_rows = BLOCK // col_dev
    total_strips = BLOCKS_DEV * sixteen_size
    block_numbers = jnp.arange(BLOCKS_DEV, dtype=jnp.int32)
    weight = observed.astype(jnp.float32)
    spread_scale = huber_scale[:, None, None]
    row_effect = jnp.zeros((fields, row_dev), jnp.float32)
    col_effect = jnp.zeros((fields, col_dev), jnp.float32)
    row_count = jnp.ones((row_dev,), jnp.float32)
    col_count = jnp.ones((col_dev,), jnp.float32)
    for sweep_number in range(SWEEPS):
        clipped = jnp.clip(
            (observations - row_effect[:, :, None] - col_effect[:, None, :]) / spread_scale,
            -HUBER_EDGE,
            HUBER_EDGE,
        )
        row_part = jnp.sum(weight[None] * clipped, axis=2)
        if sweep_number == 0:
            row_part, row_total = sum_rows((row_part, jnp.sum(weight, axis=1)))
            row_count = jnp.maximum(row_total, 1.0)
        else:
            row_part = sum_rows(row_part)
        row_effect = row_effect + huber_scale[:, None] * row_part / row_count[None, :]
        clipped = jnp.clip(
            (observations - row_effect[:, :, None] - col_effect[:, None, :]) / spread_scale,
            -HUBER_EDGE,
            HUBER_EDGE,
        )
        col_part = jnp.sum(weight[None] * clipped, axis=1)
        if sweep_number == 0:
            col_part, col_total = sum_columns((col_part, jnp.sum(weight, axis=0)))
            col_count = jnp.maximum(col_total, 1.0)
        else:
            col_part = sum_columns(col_part)
        col_effect = col_effect + huber_scale[:, None] * col_part / col_count[None, :]
    residual_field = weight[None] * (observations - row_effect[:, :, None] - col_effect[:, None, :])
    local_side = residual_field.reshape(fields, BLOCKS_DEV, BLOCK)
    row_place = (my_place * row_dev + jnp.arange(row_dev, dtype=jnp.int32)).astype(jnp.float32)
    col_place = (group_place * col_dev + jnp.arange(col_dev, dtype=jnp.int32)).astype(jnp.float32)
    location = jnp.stack([row_place[:, None] + jitter[0], col_place[None, :] + jitter[1]]).reshape(
        2, BLOCKS_DEV, BLOCK
    )
    group_map = owner_map[0]
    group_lists = neighbours[0]
    table = owned_table(group_map, sixteen_size, BLOCKS_DEV)
    my_ids = lax.dynamic_index_in_dim(table, my_place, 0, keepdims=False)
    my_targets = lax.dynamic_slice_in_dim(group_map, my_place * BLOCKS_DEV, BLOCKS_DEV)
    strip_ids = my_place * BLOCKS_DEV + block_numbers
    near_ids = lax.dynamic_slice_in_dim(group_lists, my_place * BLOCKS_DEV, BLOCKS_DEV)
    offsets = (near_ids - strip_ids[:, None] + total_strips // 2) % total_strips - total_strips // 2
    positions = (block_numbers[:, None] + REACH + offsets).reshape(-1)
    wider_places = padded(location, (("sixteen", 1),), REACH)
    near_centres = jnp.take(wider_places, positions, axis=1).reshape(
        2, BLOCKS_DEV, NEIGHBOURS, BLOCK
    )

    def tiles_of(position):
        centre = lax.dynamic_index_in_dim(location, position, 1, keepdims=False)
        beside_all = lax.dynamic_index_in_dim(near_centres, position, 1, keepdims=False)
        return covariance(
            centre, jnp.concatenate([centre[:, None], beside_all], axis=1), strip_rows
        )

    solution_now = jnp.zeros_like(local_side)
    residual_now = local_side

    def squares(observed_values):
        return lax.psum(
            jnp.sum(observed_values * observed_values, axis=(1, 2)), ("wide", "sixteen")
        )

    direction = local_side
    norm_now = squares(residual_now)
    for number in range(ITERS):
        wider = padded(direction, (("sixteen", 1),), REACH)
        near_values = jnp.take(wider, positions, axis=1).reshape(
            fields, BLOCKS_DEV, NEIGHBOURS, BLOCK
        )

        def one_block(position):
            own = lax.dynamic_index_in_dim(direction, position, 1, keepdims=False)
            beside_all = lax.dynamic_index_in_dim(near_values, position, 1, keepdims=False)
            kernel = tiles_of(position)
            stacked = jnp.concatenate([(NEIGHBOURS + 1.0) * own[:, None], beside_all], axis=1)
            return NUGGET_TERM * own + jnp.einsum("fmb,mba->fa", stacked, kernel, precision=EXACT)

        image = jnp.moveaxis(lax.map(one_block, block_numbers), 0, 1)
        alpha = norm_now / lax.psum(jnp.sum(direction * image, axis=(1, 2)), ("wide", "sixteen"))
        solution_now = solution_now + alpha[:, None, None] * direction
        residual_now = residual_now - alpha[:, None, None] * image
        if number + 1 < ITERS:
            norm_next = squares(residual_now)
            direction = residual_now + (norm_next / norm_now)[:, None, None] * direction
            norm_now = norm_next
    moved_solution, moved_residual = (
        lax.all_to_all(
            outgoing(solution_now, my_targets, sixteen_size),
            "sixteen",
            split_axis=1,
            concat_axis=1,
            tiled=True,
        ),
        lax.all_to_all(
            outgoing(residual_now, my_targets, sixteen_size),
            "sixteen",
            split_axis=1,
            concat_axis=1,
            tiled=True,
        ),
    )
    solution_now = incoming(moved_solution, my_ids, BLOCKS_DEV)
    residual_now = incoming(moved_residual, my_ids, BLOCKS_DEV)
    return (solution_now[None, None], residual_now[None, None])


def solution(mesh):
    return jax.shard_map(
        on_device,
        mesh=mesh,
        in_specs=(
            P(None, "sixteen", "wide"),
            P(),
            P("sixteen", "wide"),
            P(None, "sixteen", "wide"),
            P("wide", None),
            P("wide", None, None),
        ),
        out_specs=(P("wide", "sixteen", None, None, None), P("wide", "sixteen", None, None, None)),
        check_vma=False,
    )
```

profile of v0, /device:TPU:0, one launch (start us, length us, event | category | flops | bytes accessed | tf_op | source)
XLA Modules:
  0.0 631.3 jit_solution(12699394740307038898)
XLA Ops:
  2.2 1.7 multiply_reduce_fusion.5
  3.9 13.2 %all-reduce.2 = (f32[64,32]{1,0:T(8,128)S(1)}, f32[32]{0:T(128)S(1)}) all-reduce(f32[64,32]{1,0:T(8,128)S(1)} %multiply_reduce_fusion.5, f32[32]{0:T(128)S(1)} %get-tuple-element.242), channel_id=1, replica_groups=mesh['wide'=4,'sixteen'=8] {'wide'}, use_global_device_ids=true, to_apply=%region_3.4 | all-reduce | flops 2080 | bytes 16640 | tf_op jit(solution)/shard_map/psum | solution.py:72
  17.8 1.7 multiply_reduce_fusion.4
  19.6 37.7 %all-reduce.1 = (f32[64,128]{1,0:T(8,128)S(1)}, f32[128]{0:T(128)S(1)}) all-reduce(f32[64,128]{1,0:T(8,128)S(1)} %multiply_reduce_fusion.4, f32[128]{0:T(128)S(1)} %get-tuple-element.241), channel_id=1, replica_groups=mesh['wide'=4,'sixteen'=8] {'sixteen'}, use_global_device_ids=true, to_apply=%region_7.8 | all-reduce | flops 8320 | bytes 66560 | tf_op jit(solution)/shard_map/psum | solution.py:76
  58.0 2.0 multiply_reduce_fusion.3
  60.0 10.3 %psum.74 = f32[64,32]{1,0:T(8,128)S(1)} all-reduce(f32[64,32]{1,0:T(8,128)S(1)} %multiply_reduce_fusion.3), channel_id=1, replica_groups=mesh['wide'=4,'sixteen'=8] {'wide'}, use_global_device_ids=true, to_apply=%region_11.12 | all-reduce | flops 2048 | bytes 16384 | tf_op jit(solution)/shard_map/psum | solution.py:72
  71.1 1.8 multiply_reduce_fusion.2
  72.8 33.0 %psum.75 = f32[64,128]{1,0:T(8,128)S(1)} all-reduce(f32[64,128]{1,0:T(8,128)S(1)} %multiply_reduce_fusion.2), channel_id=1, replica_groups=mesh['wide'=4,'sixteen'=8] {'sixteen'}, use_global_device_ids=true, to_apply=%region_13.14 | all-reduce | flops 8192 | bytes 65536 | tf_op jit(solution)/shard_map/psum | solution.py:76
  106.6 2.4 multiply_reduce_fusion.1
  110.9 4.7 collective-permute-start.1
  115.8 4.7 collective-permute-start.3
  121.6 5.6 collective-permute-done.2
  127.2 2.3 collective-permute-done.3
  131.3 1.8 pad_maximum_fusion.2
  133.1 3.6 gather_fusion.1
  136.7 6.8 %broadcast_select_fusion.1 = f32[48,64,512]{2,1,0:T(8,128)} fusion(f32[48,64,512]{2,1,0:T(8,128)} %gather_fusion.1, pred[48]{0:T(512)(128)(4,1)S(1)} %get-tuple-element.279), kind=kLoop, calls=%fused_computation.120 | loop fusion | flops 1572864 | bytes 12582960 | tf_op jit(solution)/shard_map/jit(_take)/select_n | solution.py:158
  143.6 134.2 %while.24 = (s32[]{:T(128)}, f32[8,64,512]{2,1,0:T(8,128)S(1)}, s32[8]{0:T(128)S(1)}, f32[64,8,512]{2,0,1:T(8,128)}, f32[64,8,6,512]{3,0,2,1:T(8,128)}, /*index=...) while((s32[]{:T(128)}, f32[8,64,512]{2,1,0:T(8,128)S(1)}, ...), condition=%wide.region_17.19_spmd, body=%wide.region_16.18_spmd.sunk | while | flops 1444453376 | bytes 3174599 | solution.py:169
  147.4 1.2 dynamic-slice_bitcast_fusion.9
  148.5 12.0 %fusion.161 = f32[8,64,512]{2,1,0:T(8,128)S(1)} fusion(f32[8,64,512]{2,1,0:T(8,128)S(1)} %get-tuple-element.415, s32[]{:T(128)} %get-tuple-element.414, f32[512]{0:T(512)S(1)} %bitcast.164, f32[7,512]{1,0:T(8,128)S(1)} %get-tuple-element.389, f32[512]{0:T(512)S(1)} %bitcast.163, f32[7,512]{1,0:T(8,128)S(1)} %get-tuple-element.391, ...), kind=kOutput, calls=%fused_computation.38.clone.1 | convolution fusion | flops 1444413440 | bytes 1216520 | tf_op jit(solution)/shard_map/while/body/eval_jaxpr/fmb,mba->fa/dot_general | solution.py:167
  164.1 1.2 dynamic-slice_bitcast_fusion.9
  165.3 12.0 %fusion.161 = f32[8,64,512]{2,1,0:T(8,128)S(1)} fusion(f32[8,64,512]{2,1,0:T(8,128)S(1)} %get-tuple-element.415, s32[]{:T(128)} %get-tuple-element.414, f32[512]{0:T(512)S(1)} %bitcast.164, f32[7,512]{1,0:T(8,128)S(1)} %get-tuple-element.389, f32[512]{0:T(512)S(1)} %bitcast.163, f32[7,512]{1,0:T(8,128)S(1)} %get-tuple-element.391, ...), kind=kOutput, calls=%fused_computation.38.clone.1 | convolution fusion | flops 1444413440 | bytes 1216520 | tf_op jit(solution)/shard_map/while/body/eval_jaxpr/fmb,mba->fa/dot_general | solution.py:167
  180.9 1.2 dynamic-slice_bitcast_fusion.9
  182.1 12.0 %fusion.161 = f32[8,64,512]{2,1,0:T(8,128)S(1)} fusion(f32[8,64,512]{2,1,0:T(8,128)S(1)} %get-tuple-element.415, s32[]{:T(128)} %get-tuple-element.414, f32[512]{0:T(512)S(1)} %bitcast.164, f32[7,512]{1,0:T(8,128)S(1)} %get-tuple-element.389, f32[512]{0:T(512)S(1)} %bitcast.163, f32[7,512]{1,0:T(8,128)S(1)} %get-tuple-element.391, ...), kind=kOutput, calls=%fused_computation.38.clone.1 | convolution fusion | flops 1444413440 | bytes 1216520 | tf_op jit(solution)/shard_map/while/body/eval_jaxpr/fmb,mba->fa/dot_general | solution.py:167
  197.6 1.2 dynamic-slice_bitcast_fusion.9
  198.8 12.0 %fusion.161 = f32[8,64,512]{2,1,0:T(8,128)S(1)} fusion(f32[8,64,512]{2,1,0:T(8,128)S(1)} %get-tuple-element.415, s32[]{:T(128)} %get-tuple-element.414, f32[512]{0:T(512)S(1)} %bitcast.164, f32[7,512]{1,0:T(8,128)S(1)} %get-tuple-element.389, f32[512]{0:T(512)S(1)} %bitcast.163, f32[7,512]{1,0:T(8,128)S(1)} %get-tuple-element.391, ...), kind=kOutput, calls=%fused_computation.38.clone.1 | convolution fusion | flops 1444413440 | bytes 1216520 | tf_op jit(solution)/shard_map/while/body/eval_jaxpr/fmb,mba->fa/dot_general | solution.py:167
  215.6 12.0 %fusion.161 = f32[8,64,512]{2,1,0:T(8,128)S(1)} fusion(f32[8,64,512]{2,1,0:T(8,128)S(1)} %get-tuple-element.415, s32[]{:T(128)} %get-tuple-element.414, f32[512]{0:T(512)S(1)} %bitcast.164, f32[7,512]{1,0:T(8,128)S(1)} %get-tuple-element.389, f32[512]{0:T(512)S(1)} %bitcast.163, f32[7,512]{1,0:T(8,128)S(1)} %get-tuple-element.391, ...), kind=kOutput, calls=%fused_computation.38.clone.1 | convolution fusion | flops 1444413440 | bytes 1216520 | tf_op jit(solution)/shard_map/while/body/eval_jaxpr/fmb,mba->fa/dot_general | solution.py:167
  232.3 12.0 %fusion.161 = f32[8,64,512]{2,1,0:T(8,128)S(1)} fusion(f32[8,64,512]{2,1,0:T(8,128)S(1)} %get-tuple-element.415, s32[]{:T(128)} %get-tuple-element.414, f32[512]{0:T(512)S(1)} %bitcast.164, f32[7,512]{1,0:T(8,128)S(1)} %get-tuple-element.389, f32[512]{0:T(512)S(1)} %bitcast.163, f32[7,512]{1,0:T(8,128)S(1)} %get-tuple-element.391, ...), kind=kOutput, calls=%fused_computation.38.clone.1 | convolution fusion | flops 1444413440 | bytes 1216520 | tf_op jit(solution)/shard_map/while/body/eval_jaxpr/fmb,mba->fa/dot_general | solution.py:167
  247.9 1.2 dynamic-slice_bitcast_fusion.9
  249.1 12.0 %fusion.161 = f32[8,64,512]{2,1,0:T(8,128)S(1)} fusion(f32[8,64,512]{2,1,0:T(8,128)S(1)} %get-tuple-element.415, s32[]{:T(128)} %get-tuple-element.414, f32[512]{0:T(512)S(1)} %bitcast.164, f32[7,512]{1,0:T(8,128)S(1)} %get-tuple-element.389, f32[512]{0:T(512)S(1)} %bitcast.163, f32[7,512]{1,0:T(8,128)S(1)} %get-tuple-element.391, ...), kind=kOutput, calls=%fused_computation.38.clone.1 | convolution fusion | flops 1444413440 | bytes 1216520 | tf_op jit(solution)/shard_map/while/body/eval_jaxpr/fmb,mba->fa/dot_general | solution.py:167
  264.6 1.2 dynamic-slice_bitcast_fusion.9
  265.8 12.0 %fusion.161 = f32[8,64,512]{2,1,0:T(8,128)S(1)} fusion(f32[8,64,512]{2,1,0:T(8,128)S(1)} %get-tuple-element.415, s32[]{:T(128)} %get-tuple-element.414, f32[512]{0:T(512)S(1)} %bitcast.164, f32[7,512]{1,0:T(8,128)S(1)} %get-tuple-element.389, f32[512]{0:T(512)S(1)} %bitcast.163, f32[7,512]{1,0:T(8,128)S(1)} %get-tuple-element.391, ...), kind=kOutput, calls=%fused_computation.38.clone.1 | convolution fusion | flops 1444413440 | bytes 1216520 | tf_op jit(solution)/shard_map/while/body/eval_jaxpr/fmb,mba->fa/dot_general | solution.py:167
  278.6 37.1 %all-reduce = (f32[64]{0:T(128)S(1)}, f32[64]{0:T(128)S(1)}) all-reduce(f32[64]{0:T(128)S(1)} %get-tuple-element.277, f32[64]{0:T(128)S(1)} %fusion.116), channel_id=1, replica_groups=mesh['wide'=4,'sixteen'=8] {'wide','sixteen'}, use_global_device_ids=true, to_apply=%region_15.16 | all-reduce | flops 128 | bytes 1024 | tf_op jit(solution)/shard_map/psum | solution.py:150
  316.5 41.6 %psum.78 = f32[64]{0:T(128)S(1)} all-reduce(f32[64]{0:T(128)S(1)} %multiply_reduce_fusion), channel_id=1, replica_groups=mesh['wide'=4,'sixteen'=8] {'wide','sixteen'}, use_global_device_ids=true, to_apply=%region_21.23 | all-reduce | flops 64 | bytes 512 | tf_op jit(solution)/shard_map/psum | solution.py:150
  359.9 2.3 collective-permute-start.4
  362.3 2.4 collective-permute-start.5
  364.8 18.8 %collective-permute-done.4 = f32[64,4,512]{2,0,1:T(8,128)} collective-permute-done((f32[64,4,512]{2,0,1:T(8,128)S(1)}, f32[64,4,512]{2,0,1:T(8,128)}, u32[]{:S(2)}, u32[]{:S(2)}) %collective-permute-start.4) | collective-permute-done | bytes 524320 | tf_op jit(solution)/shard_map/ppermute | solution.py:28
  383.6 2.3 collective-permute-done.5
  385.9 1.8 pad_maximum_fusion.3
  387.7 3.6 gather_fusion.2
  391.3 6.9 %broadcast_select_fusion = f32[48,64,512]{2,1,0:T(8,128)} fusion(f32[48,64,512]{2,1,0:T(8,128)} %gather_fusion.2, pred[48]{0:T(512)(128)(4,1)S(1)} %get-tuple-element.279), kind=kLoop, calls=%fused_computation.119 | loop fusion | flops 1572864 | bytes 12582960 | tf_op jit(solution)/shard_map/jit(_take)/select_n | solution.py:158
  399.3 124.7 %while.25 = (s32[]{:T(128)}, f32[8,64,512]{2,1,0:T(8,128)}, s32[8]{0:T(128)S(1)}, f32[64,8,512]{2,0,1:T(8,128)S(1)}, f32[64,8,6,512]{3,0,2,1:T(8,128)}, /*index=...) while((s32[]{:T(128)}, f32[8,64,512]{2,1,0:T(8,128)}, ...), condition=%wide.region_23.25_spmd, body=%wide.region_22.24_spmd.sunk | while | flops 1444453376 | bytes 3171011 | solution.py:169
  401.9 1.2 dynamic-slice_bitcast_fusion.11
  403.1 11.8 %fusion.165 = f32[8,64,512]{2,1,0:T(8,128)} fusion(f32[8,64,512]{2,1,0:T(8,128)} %get-tuple-element.448, s32[]{:T(128)} %get-tuple-element.447, f32[512]{0:T(512)S(1)} %bitcast.166, f32[7,512]{1,0:T(8,128)S(1)} %get-tuple-element.400, f32[512]{0:T(512)S(1)} %bitcast.165, f32[7,512]{1,0:T(8,128)S(1)} %get-tuple-element.402, ...), kind=kOutput, calls=%fused_computation.96.clone.1 | convolution fusion | flops 1444413440 | bytes 1212932 | tf_op jit(solution)/shard_map/while/body/eval_jaxpr/fmb,mba->fa/dot_general | solution.py:167
  417.5 1.2 dynamic-slice_bitcast_fusion.11
  418.7 11.8 %fusion.165 = f32[8,64,512]{2,1,0:T(8,128)} fusion(f32[8,64,512]{2,1,0:T(8,128)} %get-tuple-element.448, s32[]{:T(128)} %get-tuple-element.447, f32[512]{0:T(512)S(1)} %bitcast.166, f32[7,512]{1,0:T(8,128)S(1)} %get-tuple-element.400, f32[512]{0:T(512)S(1)} %bitcast.165, f32[7,512]{1,0:T(8,128)S(1)} %get-tuple-element.402, ...), kind=kOutput, calls=%fused_computation.96.clone.1 | convolution fusion | flops 1444413440 | bytes 1212932 | tf_op jit(solution)/shard_map/while/body/eval_jaxpr/fmb,mba->fa/dot_general | solution.py:167
  433.1 1.2 dynamic-slice_bitcast_fusion.11
  434.3 11.8 %fusion.165 = f32[8,64,512]{2,1,0:T(8,128)} fusion(f32[8,64,512]{2,1,0:T(8,128)} %get-tuple-element.448, s32[]{:T(128)} %get-tuple-element.447, f32[512]{0:T(512)S(1)} %bitcast.166, f32[7,512]{1,0:T(8,128)S(1)} %get-tuple-element.400, f32[512]{0:T(512)S(1)} %bitcast.165, f32[7,512]{1,0:T(8,128)S(1)} %get-tuple-element.402, ...), kind=kOutput, calls=%fused_computation.96.clone.1 | convolution fusion | flops 1444413440 | bytes 1212932 | tf_op jit(solution)/shard_map/while/body/eval_jaxpr/fmb,mba->fa/dot_general | solution.py:167
  449.9 11.8 %fusion.165 = f32[8,64,512]{2,1,0:T(8,128)} fusion(f32[8,64,512]{2,1,0:T(8,128)} %get-tuple-element.448, s32[]{:T(128)} %get-tuple-element.447, f32[512]{0:T(512)S(1)} %bitcast.166, f32[7,512]{1,0:T(8,128)S(1)} %get-tuple-element.400, f32[512]{0:T(512)S(1)} %bitcast.165, f32[7,512]{1,0:T(8,128)S(1)} %get-tuple-element.402, ...), kind=kOutput, calls=%fused_computation.96.clone.1 | convolution fusion | flops 1444413440 | bytes 1212932 | tf_op jit(solution)/shard_map/while/body/eval_jaxpr/fmb,mba->fa/dot_general | solution.py:167
  464.3 1.2 dynamic-slice_bitcast_fusion.11
  465.5 11.8 %fusion.165 = f32[8,64,512]{2,1,0:T(8,128)} fusion(f32[8,64,512]{2,1,0:T(8,128)} %get-tuple-element.448, s32[]{:T(128)} %get-tuple-element.447, f32[512]{0:T(512)S(1)} %bitcast.166, f32[7,512]{1,0:T(8,128)S(1)} %get-tuple-element.400, f32[512]{0:T(512)S(1)} %bitcast.165, f32[7,512]{1,0:T(8,128)S(1)} %get-tuple-element.402, ...), kind=kOutput, calls=%fused_computation.96.clone.1 | convolution fusion | flops 1444413440 | bytes 1212932 | tf_op jit(solution)/shard_map/while/body/eval_jaxpr/fmb,mba->fa/dot_general | solution.py:167
  481.0 11.8 %fusion.165 = f32[8,64,512]{2,1,0:T(8,128)} fusion(f32[8,64,512]{2,1,0:T(8,128)} %get-tuple-element.448, s32[]{:T(128)} %get-tuple-element.447, f32[512]{0:T(512)S(1)} %bitcast.166, f32[7,512]{1,0:T(8,128)S(1)} %get-tuple-element.400, f32[512]{0:T(512)S(1)} %bitcast.165, f32[7,512]{1,0:T(8,128)S(1)} %get-tuple-element.402, ...), kind=kOutput, calls=%fused_computation.96.clone.1 | convolution fusion | flops 1444413440 | bytes 1212932 | tf_op jit(solution)/shard_map/while/body/eval_jaxpr/fmb,mba->fa/dot_general | solution.py:167
  496.6 11.8 %fusion.165 = f32[8,64,512]{2,1,0:T(8,128)} fusion(f32[8,64,512]{2,1,0:T(8,128)} %get-tuple-element.448, s32[]{:T(128)} %get-tuple-element.447, f32[512]{0:T(512)S(1)} %bitcast.166, f32[7,512]{1,0:T(8,128)S(1)} %get-tuple-element.400, f32[512]{0:T(512)S(1)} %bitcast.165, f32[7,512]{1,0:T(8,128)S(1)} %get-tuple-element.402, ...), kind=kOutput, calls=%fused_computation.96.clone.1 | convolution fusion | flops 1444413440 | bytes 1212932 | tf_op jit(solution)/shard_map/while/body/eval_jaxpr/fmb,mba->fa/dot_general | solution.py:167
  512.2 11.8 %fusion.165 = f32[8,64,512]{2,1,0:T(8,128)} fusion(f32[8,64,512]{2,1,0:T(8,128)} %get-tuple-element.448, s32[]{:T(128)} %get-tuple-element.447, f32[512]{0:T(512)S(1)} %bitcast.166, f32[7,512]{1,0:T(8,128)S(1)} %get-tuple-element.400, f32[512]{0:T(512)S(1)} %bitcast.165, f32[7,512]{1,0:T(8,128)S(1)} %get-tuple-element.402, ...), kind=kOutput, calls=%fused_computation.96.clone.1 | convolution fusion | flops 1444413440 | bytes 1212932 | tf_op jit(solution)/shard_map/while/body/eval_jaxpr/fmb,mba->fa/dot_general | solution.py:167
  524.0 1.5 fusion.114
  525.4 37.9 %psum.79 = f32[64]{0:T(128)S(1)} all-reduce(f32[64]{0:T(128)S(1)} %fusion.114), channel_id=1, replica_groups=mesh['wide'=4,'sixteen'=8] {'wide','sixteen'}, use_global_device_ids=true, to_apply=%region_25.27 | all-reduce | flops 64 | bytes 512 | tf_op jit(solution)/shard_map/psum | solution.py:170
  563.3 3.2 fusion.115
  567.7 1.6 copy.71
  569.3 5.3 all-to-all-start.1
  575.7 1.6 copy.68
  577.3 22.0 %all-to-all-done.1 = f32[64,8,512]{2,0,1:T(8,128)S(1)} async-done(((f32[64,8,512]{2,0,1:T(8,128)}), f32[64,8,512]{2,0,1:T(8,128)S(1)}, u32[]{:S(2)}, u32[]{:S(2)}) %all-to-all-start.1) | async-done | bytes 1048608 | tf_op jit(solution)/shard_map/all_to_all | solution.py:185
  599.3 3.6 all-to-all-start
  603.4 2.2 convolution_bitcast_fusion
  605.5 23.2 %all-to-all-done = f32[64,8,512]{2,0,1:T(8,128)S(1)} async-done(((f32[64,8,512]{2,0,1:T(8,128)}), f32[64,8,512]{2,0,1:T(8,128)S(1)}, u32[]{:S(2)}, u32[]{:S(2)}) %all-to-all-start) | async-done | bytes 1048608 | tf_op jit(solution)/shard_map/all_to_all | solution.py:178
  628.7 2.1 convolution_bitcast_fusion.2
  (182 shorter events, 41.6 us)
Async XLA Ops:
  0.6 119.9 %copy-start = (s32[1,64,6]{1,0,2:T(1,128)S(1)}, s32[1,64,6]{1,0,2:T(1,128)}, u32[]{:S(2)}) copy-start(s32[1,64,6]{1,0,2:T(1,128)} %param.17) | copy-start | bytes 4612
  3.9 111.8 %copy-start.8 = (f32[2,32,128]{2,1,0:T(8,128)S(1)}, f32[2,32,128]{2,1,0:T(8,128)}, u32[]{:S(2)}) copy-start(f32[2,32,128]{2,1,0:T(8,128)} %param.15) | copy-start | bytes 98308
  109.8 1.0 copy-start.5
  110.9 19.6 %collective-permute-start = (f32[64,4,512]{2,0,1:T(8,128)S(1)}, f32[64,4,512]{2,0,1:T(8,128)S(1)}, u32[]{:S(2)}, u32[]{:S(2)}) collective-permute-start(f32[64,4,512]{2,0,1:T(8,128)S(1)} %get-tuple-element.293), channel_id=1, source_target_pairs={{0,1},{1,2},{2,3},{3,4},{4,5},{5,6},{6,7},{7,0},{8,9},{9,10},{10,1... | collective-permute-start | bytes 1572872 | tf_op jit(solution)/shard_map/ppermute | solution.py:28
  110.9 20.4 %collective-permute-start.1 = (f32[64,4,512]{2,0,1:T(8,128)S(1)}, f32[64,4,512]{2,0,1:T(8,128)}, u32[]{:S(2)}, u32[]{:S(2)}) collective-permute-start(f32[64,4,512]{2,0,1:T(8,128)S(1)} %get-tuple-element.294), channel_id=1, source_target_pairs={{1,0},{2,1},{3,2},{4,3},{5,4},{6,5},{7,6},{0,7},{9,8},{10,9},{11,1... | collective-permute-start | bytes 1572872 | tf_op jit(solution)/shard_map/ppermute | solution.py:29
  115.8 11.4 %collective-permute-start.2 = (f32[2,4,512]{2,0,1:T(2,128)S(1)}, f32[2,4,512]{2,0,1:T(2,128)S(1)}, u32[]{:S(2)}, u32[]{:S(2)}) collective-permute-start(f32[2,4,512]{2,0,1:T(2,128)S(1)} %get-tuple-element.295), channel_id=1, source_target_pairs={{0,1},{1,2},{2,3},{3,4},{4,5},{5,6},{6,7},{7,0},{8,9},{9,10},{10,1... | collective-permute-start | bytes 49160 | tf_op jit(solution)/shard_map/ppermute | solution.py:28
  115.8 13.6 %collective-permute-start.3 = (f32[2,4,512]{2,0,1:T(2,128)S(1)}, f32[2,4,512]{2,0,1:T(2,128)S(1)}, u32[]{:S(2)}, u32[]{:S(2)}) collective-permute-start(f32[2,4,512]{2,0,1:T(2,128)S(1)} %get-tuple-element.296), channel_id=1, source_target_pairs={{1,0},{2,1},{3,2},{4,3},{5,4},{6,5},{7,6},{0,7},{9,8},{10,9},{11,1... | collective-permute-start | bytes 49160 | tf_op jit(solution)/shard_map/ppermute | solution.py:29
  130.5 0.8 copy-start.7
  277.8 105.7 %copy-start.3 = (f32[8,64,512]{2,1,0:T(8,128)}, f32[8,64,512]{2,1,0:T(8,128)S(1)}, u32[]{:S(2)}) copy-start(f32[8,64,512]{2,1,0:T(8,128)S(1)} %get-tuple-element.183) | copy-start | bytes 3145732
  277.9 86.9 %copy-start.9 = (s32[1,64]{1,0:T(1,128)S(1)}, s32[1,64]{1,0:T(1,128)}, u32[]{:S(2)}) copy-start(s32[1,64]{1,0:T(1,128)} %param.16) | copy-start | bytes 772
  358.8 1.0 copy-start.1
  359.9 23.7 %collective-permute-start.4 = (f32[64,4,512]{2,0,1:T(8,128)S(1)}, f32[64,4,512]{2,0,1:T(8,128)}, u32[]{:S(2)}, u32[]{:S(2)}) collective-permute-start(f32[64,4,512]{2,0,1:T(8,128)S(1)} %get-tuple-element.291), channel_id=1, source_target_pairs={{0,1},{1,2},{2,3},{3,4},{4,5},{5,6},{6,7},{7,0},{8,9},{9,10},{10,1... | collective-permute-start | bytes 1572872 | tf_op jit(solution)/shard_map/ppermute | solution.py:28
  362.3 23.6 %collective-permute-start.5 = (f32[64,4,512]{2,0,1:T(8,128)S(1)}, f32[64,4,512]{2,0,1:T(8,128)}, u32[]{:S(2)}, u32[]{:S(2)}) collective-permute-start(f32[64,4,512]{2,0,1:T(8,128)S(1)} %get-tuple-element.292), channel_id=1, source_target_pairs={{1,0},{2,1},{3,2},{4,3},{5,4},{6,5},{7,6},{0,7},{9,8},{10,9},{11,1... | collective-permute-start | bytes 1572872 | tf_op jit(solution)/shard_map/ppermute | solution.py:29
  391.3 8.0 %copy-start.2 = (f32[64,8,512]{2,0,1:T(8,128)S(1)}, f32[64,8,512]{2,0,1:T(8,128)}, u32[]{:S(2)}) copy-start(f32[64,8,512]{2,0,1:T(8,128)} %copy-done.1) | copy-start | bytes 3145732
  399.3 164.0 %copy-start.4 = (f32[8,64,512]{2,1,0:T(8,128)S(1)}, f32[8,64,512]{2,1,0:T(8,128)}, u32[]{:S(2)}) copy-start(f32[8,64,512]{2,1,0:T(8,128)} %copy-done.3) | copy-start | bytes 3145732
  566.5 8.0 %copy-start.6 = (f32[64,8,512]{2,0,1:T(8,128)S(1)}, f32[64,8,512]{2,0,1:T(8,128)}, u32[]{:S(2)}) copy-start(f32[64,8,512]{2,0,1:T(8,128)} %get-tuple-element.290) | copy-start | bytes 3145732
  569.3 30.1 %all-to-all-start.1 = ((f32[64,8,512]{2,0,1:T(8,128)}), f32[64,8,512]{2,0,1:T(8,128)S(1)}, u32[]{:S(2)}, u32[]{:S(2)}) async-start(f32[64,8,512]{2,0,1:T(8,128)} %copy.71), calls=%async_computation.1 | async-start | bytes 2097152 | tf_op jit(solution)/shard_map/all_to_all | solution.py:185
  599.3 29.4 %all-to-all-start = ((f32[64,8,512]{2,0,1:T(8,128)}), f32[64,8,512]{2,0,1:T(8,128)S(1)}, u32[]{:S(2)}, u32[]{:S(2)}) async-start(f32[64,8,512]{2,0,1:T(8,128)} %copy.68), calls=%async_computation | async-start | bytes 2097152 | tf_op jit(solution)/shard_map/all_to_all | solution.py:178
where the time goes:
time: 640 us; the launch traced here: 631 us
  blocking collectives  211 us (33%)
  matrix products  197 us (31%)
  waiting for transfers between devices  74.2 us (12%)
  other arithmetic  46.8 us (7%)
  local copies, waits for them, and re-layouts  46 us (7%)
  loops' own time  32.1 us (5%)
  starting transfers between devices  23.1 us (4%)
    dot_general x16, matrix products, one_block(): jnp.einsum('fmb,mba->fa', stacked, kernel, precision=EXACT)  190 us
    psum x2, blocking collectives, squares(): lax.psum(jnp.sum(observed_values * observed_values, axis=(1, 2)), ('wide'...  78.7 us
    psum x2, blocking collectives, sum_columns(): return lax.psum(observed_values, 'sixteen')  70.7 us
    psum x1, blocking collectives, on_device(): lax.psum(jnp.sum(direction * image, axis=(1, 2)), ('wide', 'sixteen'))  37.9 us
    another operation x2, loops' own time, on_device(): image = jnp.moveaxis(lax.map(one_block, block_numbers), 0, 1)  32.1 us
    ppermute x3, waiting for transfers between devices, padded(): before = lax.ppermute(last, axis, up)  24.4 us
    psum x2, blocking collectives, sum_rows(): return lax.psum(observed_values, 'wide')  23.5 us
    all_to_all x1, waiting for transfers between devices, on_device(): lax.all_to_all(outgoing(solution_now, my_targets, sixteen_size), 'sixteen...  23.2 us
  transfers between devices with their start and end apart: 8, of which 6 were waited for; matrix products, arithmetic and copies ran while one was open for 1% of the time, Pallas kernels for 0%

commit v1 on v0

v1 whole, which is shorter than its diff:
```python
import functools

import jax
import jax.numpy as jnp
from jax import lax
from jax.experimental import pallas as pl
from jax.experimental.pallas import tpu as pltpu
from jax.sharding import PartitionSpec as P

BLOCK = 512
BLOCKS_DEV = 8
REACH = 4
NEIGHBOURS = 6
SWEEPS = 2

HUBER_EDGE = 1.345
NUGGET_TERM = 1.0
SILL_TERM = 0.02
ROOT_THREE = 1.7320508075688772
LOG2E = 1.4426950408889634
GROUP = 16
MESH = pl.DeviceIdType.MESH
VMEM = pl.BlockSpec(memory_space=pltpu.VMEM)
SMEM = pl.BlockSpec(memory_space=pltpu.SMEM)


def owned_table(group_map, owners, per_owner):
    total_strips = group_map.shape[0]
    member = (group_map[None, :] == jnp.arange(owners, dtype=jnp.int32)[:, None]).astype(jnp.int32)
    ranked = jnp.cumsum(member, axis=1, dtype=jnp.int32) - 1
    slot_hit = (ranked[:, :, None] == jnp.arange(per_owner, dtype=jnp.int32)[None, None, :]).astype(
        jnp.int32
    ) * member[:, :, None]
    numbers = jnp.arange(total_strips, dtype=jnp.int32)
    return jnp.sum(slot_hit * numbers[None, :, None], axis=1, dtype=jnp.int32)


def greet(sizes):
    barrier = pltpu.get_barrier_semaphore()
    for axis, n in sizes:
        me = lax.axis_index(axis)

        def say(k, carry, axis=axis, n=n, me=me):
            pl.semaphore_signal(
                barrier, inc=1, device_id={axis: lax.rem(me + k, n)}, device_id_type=MESH
            )
            return carry

        lax.fori_loop(1, n, say, 0)
    pl.semaphore_wait(barrier, sum(n - 1 for _, n in sizes))


def all_sum(buffer, axis, n, send_sem, recv_sem):
    me = lax.axis_index(axis)

    def copy(k):
        return pltpu.make_async_remote_copy(
            src_ref=buffer.at[0],
            dst_ref=buffer.at[k],
            send_sem=send_sem.at[k],
            recv_sem=recv_sem.at[k],
            device_id={axis: lax.rem(me + k, n)},
            device_id_type=MESH,
        )

    copies = [copy(k) for k in range(1, n)]
    for c in copies:
        c.start()
    for c in copies:
        c.wait()
    total = None
    for owner in range(n):
        term = buffer[lax.rem(me - owner + n, n)]
        total = term if total is None else total + term
    return total


def swap(x):
    return pltpu.roll(x, x.shape[-1] // 2, x.ndim - 1)


def fold(x):
    return x + swap(x)


def halves(x, fields):
    return lax.broadcasted_iota(jnp.int32, x.shape, x.ndim - 1) < fields


def halo_copies(halo, rows, reach, n, send_sem, recv_sem, axis="sixteen"):
    me = lax.axis_index(axis)
    up, down = lax.rem(me + 1, n), lax.rem(me + n - 1, n)
    return [
        pltpu.make_async_remote_copy(
            src_ref=halo.at[pl.ds(rows, reach)],
            dst_ref=halo.at[pl.ds(0, reach)],
            send_sem=send_sem.at[0],
            recv_sem=recv_sem.at[0],
            device_id={axis: up},
            device_id_type=MESH,
        ),
        pltpu.make_async_remote_copy(
            src_ref=halo.at[pl.ds(reach, reach)],
            dst_ref=halo.at[pl.ds(reach + rows, reach)],
            send_sem=send_sem.at[1],
            recv_sem=recv_sem.at[1],
            device_id={axis: down},
            device_id_type=MESH,
        ),
    ]


def polish_kernel(
    nw, ns, fields, reach,
    obs, weight, scale, place, halo, place_halo, norm,
    row_eff, row_cnt, col_eff, col_cnt,
    row_buf0, row_buf1, col_buf0, col_buf1, norm_w, norm_s,
    sems_s, sems_r,
):
    rows, cols, lanes = obs.shape
    half = cols // 2
    place_rows = place.shape[0]
    place_reach = 2 * reach
    greet((("wide", nw), ("sixteen", ns)))
    place_halo[pl.ds(place_reach, place_rows)] = place[...]
    place_copies = halo_copies(
        place_halo, place_rows, place_reach, ns, sems_s.at[6], sems_r.at[6]
    )
    for c in place_copies:
        c.start()
    edge = HUBER_EDGE
    inv = 1.0 / scale[...]
    row_eff[...] = jnp.zeros_like(row_eff)
    col_eff[...] = jnp.zeros_like(col_eff)
    for sweep in range(SWEEPS):
        row_buf = (row_buf0, row_buf1)[min(sweep, 1)]
        col_buf = (col_buf0, col_buf1)[min(sweep, 1)]

        def clipped(r):
            value = (obs[r] - row_eff[pl.ds(r, 1)] - col_eff[...]) * inv
            return weight[r] * jnp.clip(value, -edge, edge)

        def row_step(r, carry):
            row_buf[0, pl.ds(r, 1)] = jnp.sum(clipped(r), axis=0, keepdims=True)
            if sweep == 0:
                row_buf[0, pl.ds(rows + r, 1)] = jnp.sum(weight[r], axis=0, keepdims=True)
            return carry

        lax.fori_loop(0, rows, row_step, 0)
        total = all_sum(row_buf, "wide", nw, sems_s.at[sweep], sems_r.at[sweep])
        if sweep == 0:
            row_cnt[...] = jnp.maximum(total[rows:], 1.0)
        row_eff[...] = row_eff[...] + scale[...] * total[:rows] / row_cnt[...]

        def col_step(r, carry):
            return carry + clipped(r)

        part = lax.fori_loop(0, rows, col_step, jnp.zeros((cols, lanes), jnp.float32))

        def packed(x):
            x = fold(x)
            low, high = x[:half], x[half:]
            return jnp.where(halves(low, fields), low, high)

        def unpacked(y):
            z = swap(y)
            first = halves(y, fields)
            return jnp.concatenate([jnp.where(first, y, z), jnp.where(first, z, y)], axis=0)

        col_buf[0, pl.ds(0, half)] = packed(part)
        if sweep == 0:
            count = lax.fori_loop(
                0, rows, lambda r, c: c + weight[r], jnp.zeros((cols, lanes), jnp.float32)
            )
            col_buf[0, pl.ds(half, half)] = packed(count)
        total = all_sum(col_buf, "sixteen", ns, sems_s.at[2 + sweep], sems_r.at[2 + sweep])
        if sweep == 0:
            col_cnt[...] = jnp.maximum(unpacked(total[half:]), 1.0)
        col_eff[...] = col_eff[...] + scale[...] * unpacked(total[:half]) / col_cnt[...]

    def rest(r, carry):
        value = weight[r] * (obs[r] - row_eff[pl.ds(r, 1)] - col_eff[...])
        halo[reach + r] = value
        return carry + jnp.sum(value * value, axis=0, keepdims=True)

    squares = lax.fori_loop(0, rows, rest, jnp.zeros((1, lanes), jnp.float32))
    copies = halo_copies(halo, rows, reach, ns, sems_s.at[7], sems_r.at[7])
    for c in copies:
        c.start()
    norm_w[0] = fold(squares)
    norm_s[0] = all_sum(norm_w, "wide", nw, sems_s.at[4], sems_r.at[4])
    norm[...] = all_sum(norm_s, "sixteen", ns, sems_s.at[5], sems_r.at[5])
    for c in copies + place_copies:
        c.wait()


def middle_kernel(
    nw, ns, reach,
    halo_in, image, dots, norm, halo, residual, alpha_out, beta_out, norm_out,
    dot_w, dot_s, norm_w, norm_s, sems_s, sems_r,
):
    rows = image.shape[0]
    lanes = image.shape[2]
    greet((("wide", nw), ("sixteen", ns)))
    dot_w[0] = fold(dots[...])
    dot_s[0] = all_sum(dot_w, "wide", nw, sems_s.at[0], sems_r.at[0])
    alpha = norm[...] / all_sum(dot_s, "sixteen", ns, sems_s.at[1], sems_r.at[1])

    def step(r, carry):
        value = halo_in[reach + r] - alpha * image[r]
        residual[r] = value
        return carry + jnp.sum(value * value, axis=0, keepdims=True)

    squares = lax.fori_loop(0, rows, step, jnp.zeros((1, lanes), jnp.float32))
    norm_w[0] = fold(squares)
    norm_s[0] = all_sum(norm_w, "wide", nw, sems_s.at[2], sems_r.at[2])
    norm_next = all_sum(norm_s, "sixteen", ns, sems_s.at[3], sems_r.at[3])
    beta = norm_next / norm[...]

    def direct(r, carry):
        halo[reach + r] = residual[r] + beta * halo_in[reach + r]
        return carry

    lax.fori_loop(0, rows, direct, 0)
    copies = halo_copies(halo, rows, reach, ns, sems_s.at[4], sems_r.at[4])
    for c in copies:
        c.start()
    alpha_out[...] = alpha
    beta_out[...] = beta
    norm_out[...] = norm_next
    for c in copies:
        c.wait()


def last_kernel(nw, ns, dots, norm, alpha_out, dot_w, dot_s, sems_s, sems_r):
    greet((("wide", nw), ("sixteen", ns)))
    dot_w[0] = fold(dots[...])
    dot_s[0] = all_sum(dot_w, "wide", nw, sems_s.at[0], sems_r.at[0])
    alpha_out[...] = norm[...] / all_sum(dot_s, "sixteen", ns, sems_s.at[1], sems_r.at[1])


def build_windows(halo, windows, starts, span, fields, strip_rows):
    blocks = windows.shape[1]
    pairs = strip_rows // 2

    def one(h, carry):
        for pair in range(pairs):
            for i, start in enumerate(starts):
                x = halo[h * pairs + pair, start : start + span, :]
                first = halves(x, fields)
                z = swap(x)
                for parity in range(2):
                    y = jnp.where(first, x, z) if parity == 0 else jnp.where(first, z, x)
                    high = y.astype(jnp.bfloat16).astype(jnp.float32)
                    both = jnp.where(first, high, y - high).astype(jnp.bfloat16)
                    at = (2 * pair + parity) * span
                    windows[i, h, at : at + span, :] = both
        return carry

    lax.fori_loop(0, blocks, one, 0)


def finish(i, acc, g, halo, image, dots, reach, fields, strip_rows):
    rows = strip_rows * GROUP
    y = fold(acc[:rows] + acc[rows:])
    pairs = strip_rows // 2
    at = pl.multiple_of(i * GROUP, GROUP)
    for pair in range(pairs):
        even = y[(2 * pair) * GROUP : (2 * pair + 1) * GROUP]
        odd = y[(2 * pair + 1) * GROUP : (2 * pair + 2) * GROUP]
        own = halo[reach + g * pairs + pair, pl.ds(at, GROUP), :]
        value = NUGGET_TERM * own + jnp.where(halves(even, fields), even, odd)
        image[pair, pl.ds(at, GROUP), :] = value
        dots[...] += jnp.sum(own * value, axis=0, keepdims=True)


def first_image_kernel(
    starts, span, reach, fields, strip_rows,
    offs, halo, others, centre, tiles, image, dots, windows,
):
    g = pl.program_id(0)
    spread = 2.0 * strip_rows
    cutoff = 6.0 * strip_rows
    wide = strip_rows * span
    rows = strip_rows * GROUP

    @pl.when(g == 0)
    def _():
        build_windows(halo, windows, starts, span, fields, strip_rows)
        dots[...] = jnp.zeros_like(dots)

    def one(i, carry):
        row_here = jnp.broadcast_to(centre[0, i, :, 0:1], (rows, wide))
        col_here = jnp.broadcast_to(centre[0, i, :, 1:2], (rows, wide))
        acc = jnp.zeros((2 * rows, 2 * fields), jnp.float32)
        for n in range(NEIGHBOURS + 1):
            h = g + REACH + offs[n]
            pair = others[h, i]
            row_gap = pair[0:1] - row_here
            col_gap = pair[1:2] - col_here
            square = row_gap * row_gap + col_gap * col_gap
            distance = square * lax.rsqrt(jnp.maximum(square, 1e-30))
            fading = jnp.maximum(1.0 - distance * (1.0 / cutoff), 0.0)
            fading = fading * fading
            fading = fading * fading
            decay = jnp.exp2(distance * (-ROOT_THREE * LOG2E / spread))
            weight = SILL_TERM * (NEIGHBOURS + 1.0 if n == 0 else 1.0)
            lead = weight * (ROOT_THREE / spread) * distance + weight
            kernel = lead * decay * fading * (1.0 + distance * (4.0 / cutoff))
            high = kernel.astype(jnp.bfloat16)
            low = (kernel - high.astype(jnp.float32)).astype(jnp.bfloat16)
            both = jnp.concatenate([high, low], axis=0)
            tiles[0, i, :, n * wide : (n + 1) * wide] = both
            acc = acc + jnp.dot(both, windows[i, h], preferred_element_type=jnp.float32)
        finish(i, acc, g, halo, image, dots, reach, fields, strip_rows)
        return carry

    lax.fori_loop(0, len(starts), one, 0)


def second_image_kernel(
    starts, span, reach, fields, strip_rows,
    offs, halo, tiles, image, dots, windows,
):
    g = pl.program_id(0)
    wide = strip_rows * span
    rows = strip_rows * GROUP

    @pl.when(g == 0)
    def _():
        build_windows(halo, windows, starts, span, fields, strip_rows)
        dots[...] = jnp.zeros_like(dots)

    def one(i, carry):
        acc = jnp.zeros((2 * rows, 2 * fields), jnp.float32)
        for n in range(NEIGHBOURS + 1):
            h = g + REACH + offs[n]
            acc = acc + jnp.dot(
                tiles[0, i, :, n * wide : (n + 1) * wide],
                windows[i, h],
                preferred_element_type=jnp.float32,
            )
        finish(i, acc, g, halo, image, dots, reach, fields, strip_rows)
        return carry

    lax.fori_loop(0, len(starts), one, 0)


def on_device(observations, huber_scale, observed, jitter, owner_map, neighbours):
    fields, row_dev, col_dev = observations.shape
    nw, ns = lax.axis_size("wide"), lax.axis_size("sixteen")
    my_place = lax.axis_index("sixteen")
    group_place = lax.axis_index("wide")
    strip_rows = BLOCK // col_dev
    total_strips = BLOCKS_DEV * ns
    rows, lanes = row_dev // 2, 2 * fields
    pairs = strip_rows // 2
    reach = REACH * pairs
    f32 = jnp.float32
    shape = jax.ShapeDtypeStruct

    def pack(x):
        return x.reshape(fields, rows, 2, col_dev).transpose(1, 3, 2, 0).reshape(rows, col_dev, lanes)

    obs = pack(observations)
    weight = pack(jnp.broadcast_to(observed.astype(f32)[None], observations.shape))
    scale = jnp.concatenate([huber_scale, huber_scale])[None]
    row_place = (my_place * row_dev + jnp.arange(row_dev, dtype=jnp.int32)).astype(f32)
    col_place = (group_place * col_dev + jnp.arange(col_dev, dtype=jnp.int32)).astype(f32)
    place = jnp.stack(
        [row_place[:, None] + jitter[0], col_place[None, :] + jitter[1]], axis=1
    )
    most = max(nw, ns)
    halo, place_halo, norm = pl.pallas_call(
        functools.partial(polish_kernel, nw, ns, fields, reach),
        out_shape=(
            shape((rows + 2 * reach, col_dev, lanes), f32),
            shape((row_dev + 4 * reach, 2, col_dev), f32),
            shape((1, lanes), f32),
        ),
        in_specs=[VMEM] * 4,
        out_specs=(VMEM,) * 3,
        scratch_shapes=[
            pltpu.VMEM((rows, lanes), f32),
            pltpu.VMEM((rows, lanes), f32),
            pltpu.VMEM((col_dev, lanes), f32),
            pltpu.VMEM((col_dev, lanes), f32),
            pltpu.VMEM((nw, 2 * rows, lanes), f32),
            pltpu.VMEM((nw, rows, lanes), f32),
            pltpu.VMEM((ns, col_dev, lanes), f32),
            pltpu.VMEM((ns, col_dev // 2, lanes), f32),
            pltpu.VMEM((nw, 1, lanes), f32),
            pltpu.VMEM((ns, 1, lanes), f32),
            pltpu.SemaphoreType.DMA((8, most)),
            pltpu.SemaphoreType.DMA((8, most)),
        ],
        compiler_params=pltpu.CompilerParams(collective_id=0, has_side_effects=True),
    )(obs, weight, scale, place)

    cut = 6 * strip_rows
    span = GROUP + 2 * cut
    starts = tuple(
        min(max(GROUP * i - cut, 0), col_dev - span) for i in range(col_dev // GROUP)
    )
    groups = len(starts)
    wide = strip_rows * span
    blocks_halo = BLOCKS_DEV + 2 * REACH
    by_block = place_halo.reshape(blocks_halo, strip_rows, 2, col_dev)
    others = jnp.stack([by_block[..., s : s + span] for s in starts], axis=1)
    others = others.transpose(0, 1, 3, 2, 4).reshape(blocks_halo, groups, 2, wide)
    centre = place.reshape(BLOCKS_DEV, strip_rows, 2, groups, GROUP)
    centre = centre.transpose(0, 3, 1, 4, 2).reshape(BLOCKS_DEV, groups, strip_rows * GROUP, 2)
    listed = (neighbours[0, 0] + total_strips // 2) % total_strips - total_strips // 2
    offs = jnp.concatenate([jnp.zeros((1,), jnp.int32), listed])

    tile_block = (1, groups, 2 * strip_rows * GROUP, (NEIGHBOURS + 1) * wide)
    tile_shape = shape((BLOCKS_DEV,) + tile_block[1:], jnp.bfloat16)
    macs = BLOCKS_DEV * groups * tile_block[2] * tile_block[3]
    whole_halo = pl.BlockSpec((rows + 2 * reach, col_dev, lanes), lambda g: (0, 0, 0))
    tile_spec = pl.BlockSpec(tile_block, lambda g: (g, 0, 0, 0))
    image_spec = pl.BlockSpec((pairs, col_dev, lanes), lambda g: (g, 0, 0))
    dots_spec = pl.BlockSpec((1, lanes), lambda g: (0, 0))
    image_shape = shape((rows, col_dev, lanes), f32)
    dots_shape = shape((1, lanes), f32)
    window_scratch = pltpu.VMEM((groups, blocks_halo, wide, lanes), jnp.bfloat16)
    static = (starts, span, reach, fields, strip_rows)
    tiles, image, dots = pl.pallas_call(
        functools.partial(first_image_kernel, *static),
        grid=(BLOCKS_DEV,),
        out_shape=(tile_shape, image_shape, dots_shape),
        in_specs=[
            SMEM,
            whole_halo,
            pl.BlockSpec((blocks_halo, groups, 2, wide), lambda g: (0, 0, 0, 0)),
            pl.BlockSpec((1, groups, strip_rows * GROUP, 2), lambda g: (g, 0, 0, 0)),
        ],
        out_specs=(tile_spec, image_spec, dots_spec),
        scratch_shapes=[window_scratch],
        cost_estimate=pl.CostEstimate(
            flops=macs * 256, bytes_accessed=macs * 2, transcendentals=macs
        ),
    )(offs, halo, others, centre)

    def mid(name_id, kernel, args, out_shape, phases, extra):
        return pl.pallas_call(
            kernel,
            out_shape=out_shape,
            in_specs=[VMEM] * len(args),
            out_specs=(VMEM,) * len(out_shape),
            scratch_shapes=[pltpu.VMEM((n, 1, lanes), f32) for _ in range(extra) for n in (nw, ns)]
            + [pltpu.SemaphoreType.DMA((phases, most))] * 2,
            compiler_params=pltpu.CompilerParams(collective_id=name_id, has_side_effects=True),
        )(*args)

    halo1, residual, alpha0, beta, norm1 = mid(
        1,
        functools.partial(middle_kernel, nw, ns, reach),
        (halo, image, dots, norm),
        (shape(halo.shape, f32), image_shape, dots_shape, dots_shape, dots_shape),
        5,
        2,
    )
    image1, dots1 = pl.pallas_call(
        functools.partial(second_image_kernel, *static),
        grid=(BLOCKS_DEV,),
        out_shape=(image_shape, dots_shape),
        in_specs=[SMEM, whole_halo, tile_spec],
        out_specs=(image_spec, dots_spec),
        scratch_shapes=[window_scratch],
        cost_estimate=pl.CostEstimate(
            flops=macs * 256, bytes_accessed=macs * 2, transcendentals=0
        ),
    )(offs, halo1, tiles)
    (alpha1,) = mid(
        2, functools.partial(last_kernel, nw, ns), (dots1, norm1), (dots_shape,), 2, 1
    )

    group_map = owner_map[0]
    table = owned_table(group_map, ns, BLOCKS_DEV)
    my_ids = lax.dynamic_index_in_dim(table, my_place, 0, keepdims=False)
    my_targets = lax.dynamic_slice_in_dim(group_map, my_place * BLOCKS_DEV, BLOCKS_DEV)
    hit = my_targets[None, :] == jnp.arange(ns, dtype=jnp.int32)[:, None]
    order = jnp.sum(hit * jnp.arange(BLOCKS_DEV, dtype=jnp.int32)[None], axis=1, dtype=jnp.int32)
    sources = my_ids // BLOCKS_DEV

    def moved(x):
        out = jnp.take(x.reshape(BLOCKS_DEV, pairs * col_dev, lanes), order, axis=0)
        got = lax.all_to_all(out, "sixteen", split_axis=0, concat_axis=0, tiled=True)
        got = jnp.take(got, sources, axis=0)
        return got.reshape(BLOCKS_DEV, pairs, col_dev, lanes)

    def unpack(x):
        x = x.reshape(BLOCKS_DEV, pairs, col_dev, 2, fields).transpose(4, 0, 1, 3, 2)
        return x.reshape(1, 1, fields, BLOCKS_DEV, BLOCK)

    start, mid_residual, last_image = (
        moved(halo[reach : reach + rows]), moved(residual), moved(image1)
    )
    solution_now = (alpha0 + alpha1 * beta) * start + alpha1 * mid_residual
    residual_now = mid_residual - alpha1 * last_image
    return unpack(solution_now), unpack(residual_now)


def solution(mesh):
    return jax.shard_map(
        on_device,
        mesh=mesh,
        in_specs=(
            P(None, "sixteen", "wide"),
            P(),
            P("sixteen", "wide"),
            P(None, "sixteen", "wide"),
            P("wide", None),
            P("wide", None, None),
        ),
        out_specs=(P("wide", "sixteen", None, None, None), P("wide", "sixteen", None, None, None)),
        check_vma=False,
    )
```

time: 640 us -> 321 us (0.50); the launches traced: 631 us -> 321 us
  Pallas kernels: 0 us -> 217 us
  matrix products: 197 us -> 0 us
  blocking collectives: 211 us -> 57.6 us
  waiting for transfers between devices: 74.2 us -> 0.01 us
  other arithmetic: 46.8 us -> 9.43 us
  loops' own time: 32.1 us -> 0 us
  starting transfers between devices: 23.1 us -> 4.43 us
  local copies, waits for them, and re-layouts: 46 us -> 31.5 us
    pallas_call x0 -> x5, Pallas kernels: none -> 217 us  [the longest x2 71.6 us: mid(): pl.pallas_call(kernel, out_shape=out_shape, in_specs=[VMEM] * len(args),...]
    psum x7 -> x0, blocking collectives: 211 us -> none  [the longest x2 78.7 us: squares(): lax.psum(jnp.sum(observed_values * observed_values, axis=(1, 2)), ('wide'...]
    dot_general x20 -> x0, matrix products: 197 us -> none  [the longest x16 190 us: one_block(): jnp.einsum('fmb,mba->fa', stacked, kernel, precision=EXACT)]
    all_to_all x0 -> x2, blocking collectives: none -> 57.6 us  [moved(): lax.all_to_all(out, 'sixteen', split_axis=0, concat_axis=0, tiled=True)]
    all_to_all x2 -> x1, waiting for transfers between devices: 45.2 us -> 0.01 us  [moved(): lax.all_to_all(out, 'sixteen', split_axis=0, concat_axis=0, tiled=True)]
    another operation x2 -> x0, loops' own time: 32.1 us -> none  [on_device(): image = jnp.moveaxis(lax.map(one_block, block_numbers), 0, 1)]
    ppermute x6 -> x0, waiting for transfers between devices: 29 us -> none  [the longest x3 24.4 us: padded(): before = lax.ppermute(last, axis, up)]
    squeeze x32 -> x2, local copies, waits for them, and re-layouts: 19.2 us -> 0.18 us  [the longest x1 0.09 us: on_device(): jitter[1]]
  transfers between devices with their start and end apart: 8 -> 1, of which waited for: 6 -> 0; matrix products, arithmetic and copies ran while one was open for 1% -> 1% of each run, Pallas kernels for 0% -> 8%
where the time goes in v1:
time: 321 us
  Pallas kernels  217 us (68%)
  blocking collectives  57.6 us (18%)
  local copies, waits for them, and re-layouts  31.5 us (10%)
  other arithmetic  9.43 us (3%)
  starting transfers between devices  4.43 us (1%)
    pallas_call x2, Pallas kernels, mid(): pl.pallas_call(kernel, out_shape=out_shape, in_specs=[VMEM] * len(args),...  71.6 us
    pallas_call x1, Pallas kernels, on_device(): pl.pallas_call(functools.partial(polish_kernel, nw, ns, fields, reach), o...  61.1 us
    all_to_all x2, blocking collectives, moved(): lax.all_to_all(out, 'sixteen', split_axis=0, concat_axis=0, tiled=True)  57.6 us
    pallas_call x1, Pallas kernels, on_device(): pl.pallas_call(functools.partial(first_image_kernel, *static), grid=(BLOC...  53.2 us
    pallas_call x1, Pallas kernels, on_device(): pl.pallas_call(functools.partial(second_image_kernel, *static), grid=(BLO...  30.8 us
  transfers between devices with their start and end apart: 1, of which 0 were waited for; matrix products, arithmetic and copies ran while one was open for 1% of the time, Pallas kernels for 8%

profile of v1, /device:TPU:0, one launch (start us, length us, event | category | flops | bytes accessed | tf_op | source)
XLA Modules:
  0.0 320.6 jit_solution(8252983121818377242)
XLA Ops:
  0.6 0.0 copy-start.4
  0.7 0.8 dynamic-slice_bitcast_fusion
  1.5 0.1 select_reduce_fusion
  1.6 0.7 fusion.12
  2.4 0.7 convert_element_type.36
  3.1 0.1 broadcast_in_dim.13
  3.2 1.3 copy.70.weight
  4.5 0.0 copy-done.4
  4.5 0.6 copy.68
  5.1 1.3 copy.69.obs
  6.4 0.0 copy-done.9
  6.4 0.6 maximum_bitcast_fusion.1.scale
  7.1 0.1 squeeze.18
  7.2 0.1 squeeze.19
  7.3 0.1 broadcast_add_fusion
  7.4 0.6 pad_maximum_fusion.place
  8.0 61.1 %shard_map.77 = (f32[32,128,128]{2,1,0:T(8,128)}, f32[64,2,128]{2,1,0:T(2,128)}, f32[1,128]{1,0:T(1,128)}) custom-call(f32[16,128,128]{2,1,0:T(8,128)} %copy.69.obs, f32[16,128,128]{2,1,0:T(8,128)} %copy.70.weight, f32[1,128]{1,0:T(1,128)} %maximum_bitcast_fusion.1.scale, f32[32,2,128]{2,1,0:T(2,128)} %pad_maximum_fusion.place), custom_call_target="tpu_custom_call" | custom-call | tf_op jit(solution)/shard_map/pallas_call | solution.py:374
  69.1 1.6 fusion.11
  71.0 0.0 copy-start.5
  71.0 0.0 copy-start
  71.0 1.1 reshape.223.others
  72.1 0.1 bitcast_add_fusion
  72.2 2.9 copy.79
  75.1 0.0 copy-done.5
  75.1 0.2 add_reduce_fusion
  75.3 0.0 copy-done
  75.3 1.0 slice.41
  76.4 0.6 pad_add_fusion.offs
  77.0 53.2 %shard_map.78 = (bf16[8,8,128,1792]{3,2,1,0:T(8,128)(2,1)}, f32[16,128,128]{2,1,0:T(8,128)}, f32[1,128]{1,0:T(1,128)}) custom-call(s32[7]{0:T(128)} %pad_add_fusion.offs, f32[32,128,128]{2,1,0:T(8,128)} %get-tuple-element.16.halo.halo_in, f32[16,8,2,256]{3,2,1,0:T(2,128)} %reshape.223.others, f32[8,8,64,2]{3,2,1,0:T(8,128)} %bitcast.83), custom_call_target="tpu_custom_call" | custom-call | flops 3758096384 | bytes 29360128 | tf_op jit(solution)/shard_map/pallas_call | solution.py:427
  130.2 45.2 %shard_map.79 = (f32[32,128,128]{2,1,0:T(8,128)}, f32[16,128,128]{2,1,0:T(8,128)}, f32[1,128]{1,0:T(1,128)}, f32[1,128]{1,0:T(1,128)}, f32[1,128]{1,0:T(1,128)}) custom-call(f32[32,128,128]{2,1,0:T(8,128)} %get-tuple-element.16.halo.halo_in, f32[16,128,128]{2,1,0:T(8,128)} %get-tuple-element.18.image, f32[1,128]{1,0:T(1,128)} %get-tuple-element.19.dots, ...), custom_call_target="tpu_custom_call" | custom-call | tf_op jit(solution)/shard_map/pallas_call | solution.py:445
  175.4 30.8 %shard_map.80 = (f32[16,128,128]{2,1,0:T(8,128)}, f32[1,128]{1,0:T(1,128)}) custom-call(s32[7]{0:T(128)} %pad_add_fusion.offs, f32[32,128,128]{2,1,0:T(8,128)} %get-tuple-element.22.halo, bf16[8,8,128,1792]{3,2,1,0:T(8,128)(2,1)} %get-tuple-element.23.tiles), custom_call_target="tpu_custom_call" | custom-call | flops 3758096384 | bytes 29360128 | tf_op jit(solution)/shard_map/pallas_call | solution.py:463
  206.2 1.9 gather_fusion.4
  208.1 0.0 copy-done.3
  208.1 0.6 gather_fusion.2
  208.8 1.8 gather_fusion
  210.6 1.3 broadcast_select_fusion.1
  211.9 28.6 %all_to_all.15 = f32[8,256,128]{2,1,0:T(8,128)S(1)} all-to-all(f32[8,256,128]{2,1,0:T(8,128)S(1)} %get-tuple-element.48), channel_id=1, replica_groups=mesh['wide'=4,'sixteen'=8] {'sixteen'}, dimensions={0} | all-to-all | bytes 2097152 | tf_op jit(solution)/shard_map/all_to_all | solution.py:488
  240.5 29.0 %all_to_all.16 = f32[8,256,128]{2,1,0:T(8,128)S(1)} all-to-all(f32[8,256,128]{2,1,0:T(8,128)S(1)} %get-tuple-element.47), channel_id=1, replica_groups=mesh['wide'=4,'sixteen'=8] {'sixteen'}, dimensions={0} | all-to-all | bytes 2097152 | tf_op jit(solution)/shard_map/all_to_all | solution.py:488
  269.5 4.4 %all-to-all-start.2 = ((f32[8,256,128]{2,1,0:T(8,128)}), f32[8,256,128]{2,1,0:T(8,128)}, u32[]{:S(2)}, u32[]{:S(2)}) async-start(f32[8,256,128]{2,1,0:T(8,128)} %get-tuple-element.46), calls=%async_computation.2 | async-start | bytes 2097152 | tf_op jit(solution)/shard_map/all_to_all | solution.py:488
  274.0 26.4 %shard_map.81 = f32[1,128]{1,0:T(1,128)} custom-call(f32[1,128]{1,0:T(1,128)} %get-tuple-element.24.dots, f32[1,128]{1,0:T(1,128)} %get-tuple-element.25.norm), custom_call_target="tpu_custom_call" | custom-call | tf_op jit(solution)/shard_map/pallas_call | solution.py:445
  300.3 0.5 broadcast.215
  300.9 0.0 copy-done.7
  300.9 0.0 copy-done.8
  300.9 1.3 add_reduce_fusion.1
  302.2 0.1 mul.68
  302.2 0.1 mul.78
  302.3 0.0 copy-done.6
  302.3 0.2 reduce_window_sum.11
  302.6 0.2 multiply_reduce_fusion
  302.8 0.6 gather_fusion.1
  303.4 0.6 gather_fusion.3
  304.1 0.0 all-to-all-done.2
  304.1 1.8 gather_fusion.5
  305.9 1.8 broadcast_select_fusion
  307.7 1.6 copy.80
  309.4 0.5 reshape.226
  309.9 0.0 copy-start.1
  310.0 1.3 copy.81
  311.3 1.7 reshape.228
  313.0 1.3 copy.83
  314.3 1.7 reshape.231
  316.1 1.3 subtract_bitcast_fusion
  317.4 1.6 copy.82
  319.0 1.6 copy.84
  (29 shorter events, 0.3 us)
Async XLA Ops:
  0.6 3.9 %copy-start.4 = (f32[64,32,128]{2,1,0:T(8,128)S(1)}, f32[64,32,128]{2,1,0:T(8,128)}, u32[]{:S(2)}) copy-start(f32[64,32,128]{2,1,0:T(8,128)} %param.8) | copy-start | bytes 3145732
  4.5 1.9 copy-start.9
  71.0 4.1 %copy-start.5 = (s32[1,64,6]{1,0,2:T(1,128)S(1)}, s32[1,64,6]{1,0,2:T(1,128)}, u32[]{:S(2)}) copy-start(s32[1,64,6]{1,0,2:T(1,128)} %param.13) | copy-start | bytes 4612
  71.0 4.3 %copy-start = (f32[32,128,128]{2,1,0:T(8,128)S(1)}, f32[32,128,128]{2,1,0:T(8,128)}, u32[]{:S(2)}) copy-start(f32[32,128,128]{2,1,0:T(8,128)} %get-tuple-element.16.halo.halo_in) | copy-start | bytes 6291460
  206.2 1.9 copy-start.3
  240.5 60.4 %copy-start.7 = (f32[1,128]{1,0:T(1,128)S(1)}, f32[1,128]{1,0:T(1,128)}, u32[]{:S(2)}) copy-start(f32[1,128]{1,0:T(1,128)} %get-tuple-element.21) | copy-start | bytes 1540
  240.5 60.4 %copy-start.8 = (f32[1,128]{1,0:T(1,128)S(1)}, f32[1,128]{1,0:T(1,128)}, u32[]{:S(2)}) copy-start(f32[1,128]{1,0:T(1,128)} %get-tuple-element.26) | copy-start | bytes 1540
  240.5 61.8 %copy-start.6 = (s32[1,64]{1,0:T(1,128)S(1)}, s32[1,64]{1,0:T(1,128)}, u32[]{:S(2)}) copy-start(s32[1,64]{1,0:T(1,128)} %param.12) | copy-start | bytes 772
  269.5 34.5 %all-to-all-start.2 = ((f32[8,256,128]{2,1,0:T(8,128)}), f32[8,256,128]{2,1,0:T(8,128)}, u32[]{:S(2)}, u32[]{:S(2)}) async-start(f32[8,256,128]{2,1,0:T(8,128)} %get-tuple-element.46), calls=%async_computation.2 | async-start | bytes 2097152 | tf_op jit(solution)/shard_map/all_to_all | solution.py:488
  307.7 2.2 copy-start.2
  309.9 3.1 copy-start.1

commit v2 on v1

--- a/solution.py
+++ b/solution.py
@@ -129,6 +129,9 @@
     for c in place_copies:
         c.start()
     edge = HUBER_EDGE
+    diagonal = lax.broadcasted_iota(jnp.int32, (cols, lanes), 0) == lax.broadcasted_iota(
+        jnp.int32, (cols, lanes), 1
+    )
     inv = 1.0 / scale[...]
     row_eff[...] = jnp.zeros_like(row_eff)
     col_eff[...] = jnp.zeros_like(col_eff)
@@ -169,13 +172,18 @@
 
         col_buf[0, pl.ds(0, half)] = packed(part)
         if sweep == 0:
+            col_buf[0, pl.ds(half, 8)] = jnp.zeros((8, lanes), jnp.float32)
             count = lax.fori_loop(
                 0, rows, lambda r, c: c + weight[r], jnp.zeros((cols, lanes), jnp.float32)
             )
-            col_buf[0, pl.ds(half, half)] = packed(count)
+            col_buf[0, pl.ds(half, 1)] = jnp.sum(
+                jnp.where(diagonal, fold(count), 0.0), axis=0, keepdims=True
+            )
         total = all_sum(col_buf, "sixteen", ns, sems_s.at[2 + sweep], sems_r.at[2 + sweep])
         if sweep == 0:
-            col_cnt[...] = jnp.maximum(unpacked(total[half:]), 1.0)
+            spread = jnp.where(diagonal, jnp.broadcast_to(total[half : half + 1], (cols, lanes)), 0.0)
+            count = jnp.sum(spread, axis=1, keepdims=True)
+            col_cnt[...] = jnp.maximum(jnp.broadcast_to(count, (cols, lanes)), 1.0)
         col_eff[...] = col_eff[...] + scale[...] * unpacked(total[:half]) / col_cnt[...]
 
     def rest(r, carry):
@@ -196,7 +204,7 @@
 
 def middle_kernel(
     nw, ns, reach,
-    halo_in, image, dots, norm, halo, residual, alpha_out, beta_out, norm_out,
+    row_map, halo_in, image, dots, norm, halo, residual, alpha_out, beta_out, norm_out,
     dot_w, dot_s, norm_w, norm_s, sems_s, sems_r,
 ):
     rows = image.shape[0]
@@ -207,7 +215,7 @@
     alpha = norm[...] / all_sum(dot_s, "sixteen", ns, sems_s.at[1], sems_r.at[1])
 
     def step(r, carry):
-        value = halo_in[reach + r] - alpha * image[r]
+        value = halo_in[reach + r] - alpha * image[row_map[r]]
         residual[r] = value
         return carry + jnp.sum(value * value, axis=0, keepdims=True)
 
@@ -230,13 +238,6 @@
     norm_out[...] = norm_next
     for c in copies:
         c.wait()
-
-
-def last_kernel(nw, ns, dots, norm, alpha_out, dot_w, dot_s, sems_s, sems_r):
-    greet((("wide", nw), ("sixteen", ns)))
-    dot_w[0] = fold(dots[...])
-    dot_s[0] = all_sum(dot_w, "wide", nw, sems_s.at[0], sems_r.at[0])
-    alpha_out[...] = norm[...] / all_sum(dot_s, "sixteen", ns, sems_s.at[1], sems_r.at[1])
 
 
 def build_windows(halo, windows, starts, span, fields, strip_rows):
@@ -260,25 +261,53 @@
     lax.fori_loop(0, blocks, one, 0)
 
 
-def finish(i, acc, g, halo, image, dots, reach, fields, strip_rows):
+def finish(i, acc, own_of, store, dots, fields, strip_rows):
     rows = strip_rows * GROUP
     y = fold(acc[:rows] + acc[rows:])
-    pairs = strip_rows // 2
     at = pl.multiple_of(i * GROUP, GROUP)
-    for pair in range(pairs):
+    for pair in range(strip_rows // 2):
         even = y[(2 * pair) * GROUP : (2 * pair + 1) * GROUP]
         odd = y[(2 * pair + 1) * GROUP : (2 * pair + 2) * GROUP]
-        own = halo[reach + g * pairs + pair, pl.ds(at, GROUP), :]
+        own = own_of(pair, at)
         value = NUGGET_TERM * own + jnp.where(halves(even, fields), even, odd)
-        image[pair, pl.ds(at, GROUP), :] = value
+        store(pair, at, value)
         dots[...] += jnp.sum(own * value, axis=0, keepdims=True)
 
 
+def shifted(staged, received, n, send_sem, recv_sem):
+    me = lax.axis_index("sixteen")
+    return [pltpu.make_async_copy(staged.at[0], received.at[0], send_sem.at[0])] + [
+        pltpu.make_async_remote_copy(
+            src_ref=staged.at[k],
+            dst_ref=received.at[k],
+            send_sem=send_sem.at[k],
+            recv_sem=recv_sem.at[k],
+            device_id={"sixteen": lax.rem(me + k, n)},
+            device_id_type=MESH,
+        )
+        for k in range(1, n)
+    ]
+
+
+def stage(staged, source, first, chosen):
+    slots, pairs = staged.shape[:2]
+
+    def one(k, carry):
+        for pair in range(pairs):
+            staged[k, pair] = source[first + chosen[k] * pairs + pair]
+        return carry
+
+    lax.fori_loop(0, slots, one, 0)
+
+
 def first_image_kernel(
-    starts, span, reach, fields, strip_rows,
-    offs, halo, others, centre, tiles, image, dots, windows,
+    ns, starts, span, reach, fields, strip_rows,
+    offs, step_block, chosen, halo, others, centre,
+    tiles, image, dots, received,
+    windows, staged, send_sem, recv_sem,
 ):
     g = pl.program_id(0)
+    pairs = strip_rows // 2
     spread = 2.0 * strip_rows
     cutoff = 6.0 * strip_rows
     wide = strip_rows * span
@@ -286,15 +315,22 @@
 
     @pl.when(g == 0)
     def _():
+        stage(staged, halo, reach, chosen)
+        greet((("sixteen", ns),))
+        for c in shifted(staged, received, ns, send_sem, recv_sem):
+            c.start()
         build_windows(halo, windows, starts, span, fields, strip_rows)
         dots[...] = jnp.zeros_like(dots)
 
+    block = step_block[g]
+
     def one(i, carry):
-        row_here = jnp.broadcast_to(centre[0, i, :, 0:1], (rows, wide))
-        col_here = jnp.broadcast_to(centre[0, i, :, 1:2], (rows, wide))
+        here = centre[block, i]
+        row_here = jnp.broadcast_to(here[:, 0:1], (rows, wide))
+        col_here = jnp.broadcast_to(here[:, 1:2], (rows, wide))
         acc = jnp.zeros((2 * rows, 2 * fields), jnp.float32)
         for n in range(NEIGHBOURS + 1):
-            h = g + REACH + offs[n]
+            h = block + REACH + offs[n]
             pair = others[h, i]
             row_gap = pair[0:1] - row_here
             col_gap = pair[1:2] - col_here
@@ -312,38 +348,111 @@
             both = jnp.concatenate([high, low], axis=0)
             tiles[0, i, :, n * wide : (n + 1) * wide] = both
             acc = acc + jnp.dot(both, windows[i, h], preferred_element_type=jnp.float32)
-        finish(i, acc, g, halo, image, dots, reach, fields, strip_rows)
+
+        def store(pair, at, value):
+            image[pair, pl.ds(at, GROUP), :] = value
+
+        def own_of(pair, at):
+            return halo[reach + block * pairs + pair, pl.ds(at, GROUP), :]
+
+        finish(i, acc, own_of, store, dots, fields, strip_rows)
         return carry
 
     lax.fori_loop(0, len(starts), one, 0)
 
+    @pl.when(g == pl.num_programs(0) - 1)
+    def _():
+        for c in shifted(staged, received, ns, send_sem, recv_sem):
+            c.wait()
+
 
 def second_image_kernel(
-    starts, span, reach, fields, strip_rows,
-    offs, halo, tiles, image, dots, windows,
+    nw, ns, starts, span, reach, fields, strip_rows,
+    offs, step_block, chosen, halo, residual, norm, tiles,
+    alpha, received_residual, received_image,
+    windows, dots, staged, staged_image, local_image, dot_w, dot_s,
+    send_sem, recv_sem, send_image, recv_image, sems_s, sems_r,
 ):
     g = pl.program_id(0)
+    last = pl.num_programs(0) - 1
+    pairs = strip_rows // 2
     wide = strip_rows * span
     rows = strip_rows * GROUP
+    by_owner = ns == BLOCKS_DEV
 
     @pl.when(g == 0)
     def _():
+        stage(staged, residual, 0, chosen)
+        greet((("wide", nw), ("sixteen", ns)))
+        for c in shifted(staged, received_residual, ns, send_sem, recv_sem):
+            c.start()
         build_windows(halo, windows, starts, span, fields, strip_rows)
         dots[...] = jnp.zeros_like(dots)
+
+    block = step_block[g]
+    slot = lax.rem(g + 1, BLOCKS_DEV) if by_owner else g
 
     def one(i, carry):
         acc = jnp.zeros((2 * rows, 2 * fields), jnp.float32)
         for n in range(NEIGHBOURS + 1):
-            h = g + REACH + offs[n]
+            h = block + REACH + offs[n]
             acc = acc + jnp.dot(
                 tiles[0, i, :, n * wide : (n + 1) * wide],
                 windows[i, h],
                 preferred_element_type=jnp.float32,
             )
-        finish(i, acc, g, halo, image, dots, reach, fields, strip_rows)
+
+        def store(pair, at, value):
+            if by_owner:
+                staged_image[slot, pair, pl.ds(at, GROUP), :] = value
+            else:
+                local_image[slot * pairs + pair, pl.ds(at, GROUP), :] = value
+
+        def own_of(pair, at):
+            return halo[reach + block * pairs + pair, pl.ds(at, GROUP), :]
+
+        finish(i, acc, own_of, store, dots, fields, strip_rows)
         return carry
 
     lax.fori_loop(0, len(starts), one, 0)
+    images = shifted(staged_image, received_image, ns, send_image, recv_image)
+    if by_owner:
+        for k in range(ns):
+
+            @pl.when(g == (k - 1) % ns)
+            def _(k=k):
+                images[k].start()
+
+    @pl.when(g == last)
+    def _():
+        if not by_owner:
+            stage(staged_image, local_image, 0, chosen)
+            for c in images:
+                c.start()
+        dot_w[0] = fold(dots[...])
+        dot_s[0] = all_sum(dot_w, "wide", nw, sems_s.at[0], sems_r.at[0])
+        alpha[...] = norm[...] / all_sum(dot_s, "sixteen", ns, sems_s.at[1], sems_r.at[1])
+        for c in shifted(staged, received_residual, ns, send_sem, recv_sem):
+            c.wait()
+        for c in images:
+            c.wait()
+
+
+def final_kernel(fields, strip_rows, came, start, residual, image, alpha0, alpha1, beta, out, rest):
+    pairs, cols = start.shape[1:3]
+    lead = alpha0[...] + alpha1[...] * beta[...]
+    step = alpha1[...]
+    for j in range(BLOCKS_DEV):
+        k = came[j]
+        for pair in range(pairs):
+            value = residual[k, pair]
+            first = (lead * start[k, pair] + step * value).T
+            second = (value - step * image[k, pair]).T
+            for parity in range(2):
+                at = (2 * pair + parity) * cols
+                part = slice(parity * fields, (parity + 1) * fields)
+                out[:, j, at : at + cols] = first[part]
+                rest[:, j, at : at + cols] = second[part]
 
 
 def on_device(observations, huber_scale, observed, jitter, owner_map, neighbours):
@@ -387,7 +496,7 @@
             pltpu.VMEM((col_dev, lanes), f32),
             pltpu.VMEM((nw, 2 * rows, lanes), f32),
             pltpu.VMEM((nw, rows, lanes), f32),
-            pltpu.VMEM((ns, col_dev, lanes), f32),
+            pltpu.VMEM((ns, col_dev // 2 + 8, lanes), f32),
             pltpu.VMEM((ns, col_dev // 2, lanes), f32),
             pltpu.VMEM((nw, 1, lanes), f32),
             pltpu.VMEM((ns, 1, lanes), f32),
@@ -415,7 +524,6 @@
 
     tile_block = (1, groups, 2 * strip_rows * GROUP, (NEIGHBOURS + 1) * wide)
     tile_shape = shape((BLOCKS_DEV,) + tile_block[1:], jnp.bfloat16)
-    macs = BLOCKS_DEV * groups * tile_block[2] * tile_block[3]
     whole_halo = pl.BlockSpec((rows + 2 * reach, col_dev, lanes), lambda g: (0, 0, 0))
     tile_spec = pl.BlockSpec(tile_block, lambda g: (g, 0, 0, 0))
     image_spec = pl.BlockSpec((pairs, col_dev, lanes), lambda g: (g, 0, 0))
@@ -424,28 +532,49 @@
     dots_shape = shape((1, lanes), f32)
     window_scratch = pltpu.VMEM((groups, blocks_halo, wide, lanes), jnp.bfloat16)
     static = (starts, span, reach, fields, strip_rows)
-    tiles, image, dots = pl.pallas_call(
-        functools.partial(first_image_kernel, *static),
+    group_map = owner_map[0]
+    numbers = jnp.arange(BLOCKS_DEV, dtype=jnp.int32)
+    table = owned_table(group_map, ns, BLOCKS_DEV)
+    my_ids = lax.dynamic_index_in_dim(table, my_place, 0, keepdims=False)
+    my_targets = lax.dynamic_slice_in_dim(group_map, my_place * BLOCKS_DEV, BLOCKS_DEV)
+    owners = (my_place + jnp.arange(ns, dtype=jnp.int32)) % ns
+    hit = my_targets[None, :] == owners[:, None]
+    chosen = jnp.sum(hit * numbers[None], axis=1, dtype=jnp.int32)
+    came = (my_place - my_ids // BLOCKS_DEV + ns) % ns
+    if ns == BLOCKS_DEV:
+        step_block = jnp.roll(chosen, -1)
+        step_of = jnp.sum(
+            (step_block[None, :] == numbers[:, None]) * numbers[None], axis=1, dtype=jnp.int32
+        )
+    else:
+        step_block = step_of = numbers
+    row_map = (step_of[:, None] * pairs + jnp.arange(pairs, dtype=jnp.int32)[None]).reshape(-1)
+    anywhere = pl.BlockSpec(memory_space=pl.ANY)
+    moved_shape = shape((ns, pairs, col_dev, lanes), f32)
+    staging = pltpu.VMEM(moved_shape.shape, f32)
+
+    tiles, image, dots, start = pl.pallas_call(
+        functools.partial(first_image_kernel, ns, *static),
         grid=(BLOCKS_DEV,),
-        out_shape=(tile_shape, image_shape, dots_shape),
+        out_shape=(tile_shape, image_shape, dots_shape, moved_shape),
         in_specs=[
+            SMEM,
+            SMEM,
             SMEM,
             whole_halo,
             pl.BlockSpec((blocks_halo, groups, 2, wide), lambda g: (0, 0, 0, 0)),
-            pl.BlockSpec((1, groups, strip_rows * GROUP, 2), lambda g: (g, 0, 0, 0)),
+            pl.BlockSpec((BLOCKS_DEV, groups, strip_rows * GROUP, 2), lambda g: (0, 0, 0, 0)),
         ],
-        out_specs=(tile_spec, image_spec, dots_spec),
-        scratch_shapes=[window_scratch],
-        cost_estimate=pl.CostEstimate(
-            flops=macs * 256, bytes_accessed=macs * 2, transcendentals=macs
-        ),
-    )(offs, halo, others, centre)
+        out_specs=(tile_spec, image_spec, dots_spec, anywhere),
+        scratch_shapes=[window_scratch, staging] + [pltpu.SemaphoreType.DMA((ns,))] * 2,
+        compiler_params=pltpu.CompilerParams(collective_id=3, has_side_effects=True),
+    )(offs, step_block, chosen, halo, others, centre)
 
     def mid(name_id, kernel, args, out_shape, phases, extra):
         return pl.pallas_call(
             kernel,
             out_shape=out_shape,
-            in_specs=[VMEM] * len(args),
+            in_specs=[SMEM] + [VMEM] * (len(args) - 1),
             out_specs=(VMEM,) * len(out_shape),
             scratch_shapes=[pltpu.VMEM((n, 1, lanes), f32) for _ in range(extra) for n in (nw, ns)]
             + [pltpu.SemaphoreType.DMA((phases, most))] * 2,
@@ -455,50 +584,47 @@
     halo1, residual, alpha0, beta, norm1 = mid(
         1,
         functools.partial(middle_kernel, nw, ns, reach),
-        (halo, image, dots, norm),
+        (row_map, halo, image, dots, norm),
         (shape(halo.shape, f32), image_shape, dots_shape, dots_shape, dots_shape),
         5,
         2,
     )
-    image1, dots1 = pl.pallas_call(
-        functools.partial(second_image_kernel, *static),
+    alpha1, mid_residual, last_image = pl.pallas_call(
+        functools.partial(second_image_kernel, nw, ns, *static),
         grid=(BLOCKS_DEV,),
-        out_shape=(image_shape, dots_shape),
-        in_specs=[SMEM, whole_halo, tile_spec],
-        out_specs=(image_spec, dots_spec),
-        scratch_shapes=[window_scratch],
-        cost_estimate=pl.CostEstimate(
-            flops=macs * 256, bytes_accessed=macs * 2, transcendentals=0
-        ),
-    )(offs, halo1, tiles)
-    (alpha1,) = mid(
-        2, functools.partial(last_kernel, nw, ns), (dots1, norm1), (dots_shape,), 2, 1
-    )
-
-    group_map = owner_map[0]
-    table = owned_table(group_map, ns, BLOCKS_DEV)
-    my_ids = lax.dynamic_index_in_dim(table, my_place, 0, keepdims=False)
-    my_targets = lax.dynamic_slice_in_dim(group_map, my_place * BLOCKS_DEV, BLOCKS_DEV)
-    hit = my_targets[None, :] == jnp.arange(ns, dtype=jnp.int32)[:, None]
-    order = jnp.sum(hit * jnp.arange(BLOCKS_DEV, dtype=jnp.int32)[None], axis=1, dtype=jnp.int32)
-    sources = my_ids // BLOCKS_DEV
-
-    def moved(x):
-        out = jnp.take(x.reshape(BLOCKS_DEV, pairs * col_dev, lanes), order, axis=0)
-        got = lax.all_to_all(out, "sixteen", split_axis=0, concat_axis=0, tiled=True)
-        got = jnp.take(got, sources, axis=0)
-        return got.reshape(BLOCKS_DEV, pairs, col_dev, lanes)
-
-    def unpack(x):
-        x = x.reshape(BLOCKS_DEV, pairs, col_dev, 2, fields).transpose(4, 0, 1, 3, 2)
-        return x.reshape(1, 1, fields, BLOCKS_DEV, BLOCK)
-
-    start, mid_residual, last_image = (
-        moved(halo[reach : reach + rows]), moved(residual), moved(image1)
-    )
-    solution_now = (alpha0 + alpha1 * beta) * start + alpha1 * mid_residual
-    residual_now = mid_residual - alpha1 * last_image
-    return unpack(solution_now), unpack(residual_now)
+        out_shape=(dots_shape, moved_shape, moved_shape),
+        in_specs=[
+            SMEM,
+            SMEM,
+            SMEM,
+            whole_halo,
+            pl.BlockSpec((rows, col_dev, lanes), lambda g: (0, 0, 0)),
+            dots_spec,
+            tile_spec,
+        ],
+        out_specs=(dots_spec, anywhere, anywhere),
+        scratch_shapes=[
+            window_scratch,
+            pltpu.VMEM((1, lanes), f32),
+            staging,
+            staging,
+            pltpu.VMEM((8, 128) if ns == BLOCKS_DEV else (rows, col_dev, lanes), f32),
+            pltpu.VMEM((nw, 1, lanes), f32),
+            pltpu.VMEM((ns, 1, lanes), f32),
+        ]
+        + [pltpu.SemaphoreType.DMA((ns,))] * 4
+        + [pltpu.SemaphoreType.DMA((2, most))] * 2,
+        compiler_params=pltpu.CompilerParams(collective_id=2, has_side_effects=True),
+    )(offs, step_block, chosen, halo1, residual, norm1, tiles)
+
+    out_shape = shape((fields, BLOCKS_DEV, BLOCK), f32)
+    solution_now, residual_now = pl.pallas_call(
+        functools.partial(final_kernel, fields, strip_rows),
+        out_shape=(out_shape, out_shape),
+        in_specs=[SMEM] + [VMEM] * 6,
+        out_specs=(VMEM, VMEM),
+    )(came, start, mid_residual, last_image, alpha0, alpha1, beta)
+    return solution_now[None, None], residual_now[None, None]
 
 
 def solution(mesh):

time: 321 us -> 237 us (0.74)
  blocking collectives: 57.6 us -> 0 us
  local copies, waits for them, and re-layouts: 31.5 us -> 11.4 us
  starting transfers between devices: 4.43 us -> 0 us
    all_to_all x2 -> x0, blocking collectives: 57.6 us -> none  [moved(): lax.all_to_all(out, 'sixteen', split_axis=0, concat_axis=0, tiled=True)]
    gather x6 -> x0, local copies, waits for them, and re-layouts: 7.45 us -> none  [the longest x3 4.38 us: moved(): out = jnp.take(x.reshape(BLOCKS_DEV, pairs * col_dev, lanes), order, axis=0)]
    pallas_call x4, Pallas kernels: 156 us -> 162 us  [the longest x1 58.7 us: on_device(): pl.pallas_call(functools.partial(first_image_kernel, ns, *static), grid=(...]
    pallas_call x1, Pallas kernels: 61.1 us -> 55.5 us  [on_device(): pl.pallas_call(functools.partial(polish_kernel, nw, ns, fields, reach), o...]
    all_to_all x1 -> x0, starting transfers between devices: 4.43 us -> none  [moved(): lax.all_to_all(out, 'sixteen', split_axis=0, concat_axis=0, tiled=True)]
    select_n x3 -> x0, local copies, waits for them, and re-layouts: 4.26 us -> none  [moved(): got = jnp.take(got, sources, axis=0)]
    reshape x3 -> x0, local copies, waits for them, and re-layouts: 4.02 us -> none  [moved(): return got.reshape(BLOCKS_DEV, pairs, col_dev, lanes)]
  transfers between devices with their start and end apart: 1 -> 0, of which waited for: 0 -> 0; matrix products, arithmetic and copies ran while one was open for 1% -> 0% of each run, Pallas kernels for 8% -> 0%
where the time goes in v2:
time: 237 us; the launch traced here: 236 us
  Pallas kernels  217 us (92%)
  local copies, waits for them, and re-layouts  11.4 us (5%)
  other arithmetic  6.64 us (3%)
    pallas_call x1, Pallas kernels, on_device(): pl.pallas_call(functools.partial(first_image_kernel, ns, *static), grid=(...  58.7 us
    pallas_call x1, Pallas kernels, on_device(): pl.pallas_call(functools.partial(polish_kernel, nw, ns, fields, reach), o...  55.5 us
    pallas_call x1, Pallas kernels, on_device(): pl.pallas_call(functools.partial(second_image_kernel, nw, ns, *static), g...  54.4 us
    pallas_call x1, Pallas kernels, mid(): pl.pallas_call(kernel, out_shape=out_shape, in_specs=[SMEM] + [VMEM] * (l...  43.3 us
    pallas_call x1, Pallas kernels, on_device(): pl.pallas_call(functools.partial(final_kernel, fields, strip_rows), out_s...  5.51 us

profile of v2, /device:TPU:0, one launch (start us, length us, event | category | flops | bytes accessed | tf_op | source)
XLA Modules:
  0.0 236.3 jit_solution(18223021596245088693)
XLA Ops:
  0.6 0.7 dynamic-slice_bitcast_fusion
  1.4 1.4 maximum_bitcast_fusion.1.scale
  2.8 0.9 add_reduce_fusion
  3.7 0.6 pad_add_fusion.offs
  4.3 0.7 fusion.8
  5.0 0.2 reduce_window_sum.11
  5.2 0.2 multiply_reduce_fusion
  5.4 0.6 and_select_fusion
  6.0 0.2 select_reduce_fusion.1.chosen
  6.1 0.0 copy-start.1
  6.1 0.1 slice.38
  6.2 0.1 pad_add_fusion.1.step_block
  6.3 0.0 copy-start.2
  6.3 0.1 select_reduce_fusion
  6.5 0.1 iota_add_fusion
  6.5 0.7 add.180.row_map
  7.2 0.7 convert_element_type.38
  7.9 0.7 fusion.14
  8.6 0.1 broadcast_add_fusion
  8.8 0.6 pad_maximum_fusion.place
  9.4 0.1 squeeze.19
  9.5 0.1 squeeze.20
  9.6 0.0 copy-start
  9.6 0.1 bitcast_add_fusion
  9.7 0.1 broadcast_in_dim.11
  9.8 1.3 copy.43.weight
  11.1 0.0 copy-done.1
  11.1 0.0 copy-done.2
  11.1 0.0 copy-done
  11.1 0.6 copy.41
  11.7 1.3 copy.42.obs
  13.0 55.5 %shard_map.77 = (f32[32,128,128]{2,1,0:T(8,128)}, f32[64,2,128]{2,1,0:T(2,128)}, f32[1,128]{1,0:T(1,128)}) custom-call(f32[16,128,128]{2,1,0:T(8,128)} %copy.42.obs, f32[16,128,128]{2,1,0:T(8,128)} %copy.43.weight, f32[1,128]{1,0:T(1,128)} %maximum_bitcast_fusion.1.scale, f32[32,2,128]{2,1,0:T(2,128)} %pad_maximum_fusion.place), custom_call_target="tpu_custom_call" | custom-call | tf_op jit(solution)/shard_map/pallas_call | solution.py:483
  68.6 1.5 fusion.13
  70.3 1.1 reshape.204.others
  71.4 2.9 %copy.52 = f32[8,8,4,16,2]{4,3,2,1,0:T(8,128)} copy(f32[8,8,4,16,2]{3,1,4,2,0:T(8,128)S(1)} %maximum_bitcast_fusion) | data formatting | bytes 65536 | tf_op jit(solution)/shard_map/transpose | solution.py:521
  74.3 58.7 %shard_map.78 = (bf16[8,8,128,1792]{3,2,1,0:T(8,128)(2,1)}, f32[16,128,128]{2,1,0:T(8,128)}, f32[1,128]{1,0:T(1,128)}, f32[8,2,128,128]{3,2,1,0:T(8,128)}) custom-call(s32[7]{0:T(128)} %pad_add_fusion.offs, s32[8]{0:T(128)} %copy-done.2, s32[8]{0:T(128)} %copy-done.1, f32[32,128,128]{2,1,0:T(8,128)} %get-tuple-element.19.halo.halo_in, ...), custom_call_target="tpu_custom_call" | custom-call | tf_op jit(solution)/shard_map/pallas_call | solution.py:556
  133.0 43.3 %shard_map.79 = (f32[32,128,128]{2,1,0:T(8,128)}, f32[16,128,128]{2,1,0:T(8,128)}, f32[1,128]{1,0:T(1,128)}, f32[1,128]{1,0:T(1,128)}, f32[1,128]{1,0:T(1,128)}) custom-call(s32[16]{0:T(128)} %add.180.row_map, f32[32,128,128]{2,1,0:T(8,128)} %get-tuple-element.19.halo.halo_in, f32[16,128,128]{2,1,0:T(8,128)} %get-tuple-element.22.image, ...), custom_call_target="tpu_custom_call" | custom-call | tf_op jit(solution)/shard_map/pallas_call | solution.py:574
  176.3 54.4 %shard_map.80 = (f32[1,128]{1,0:T(1,128)}, f32[8,2,128,128]{3,2,1,0:T(8,128)}, f32[8,2,128,128]{3,2,1,0:T(8,128)}) custom-call(s32[7]{0:T(128)} %pad_add_fusion.offs, s32[8]{0:T(128)} %copy-done.2, s32[8]{0:T(128)} %copy-done.1, f32[32,128,128]{2,1,0:T(8,128)} %get-tuple-element.25.halo, f32[16,128,128]{2,1,0:T(8,128)} %get-tuple-element.26.residual, ...), custom_call_target="tpu_custom_call" | custom-call | tf_op jit(solution)/shard_map/pallas_call | solution.py:592
  230.8 5.5 %shard_map.81 = (f32[64,8,512]{2,1,0:T(8,128)}, f32[64,8,512]{2,1,0:T(8,128)}) custom-call(s32[8]{0:T(128)} %get-tuple-element.45.came, f32[8,2,128,128]{3,2,1,0:T(8,128)} %get-tuple-element.21.start, f32[8,2,128,128]{3,2,1,0:T(8,128)} %get-tuple-element.29.residual, f32[8,2,128,128]{3,2,1,0:T(8,128)} %get-tuple-element.30.image, ...), custom_call_target="tpu_custom_call" | custom-call | tf_op jit(solution)/shard_map/pallas_call | solution.py:621
  (16 shorter events, 0.3 us)
Async XLA Ops:
  6.1 5.0 %copy-start.1 = (s32[8]{0:T(128)}, s32[8]{0:T(128)S(1)}, u32[]{:S(2)}) copy-start(s32[8]{0:T(128)S(1)} %select_reduce_fusion.1.chosen) | copy-start | bytes 100
  6.3 4.8 %copy-start.2 = (s32[8]{0:T(128)}, s32[8]{0:T(128)S(1)}, u32[]{:S(2)}) copy-start(s32[8]{0:T(128)S(1)} %pad_add_fusion.1.step_block) | copy-start | bytes 100
  9.6 1.5 copy-start

commit v3 on v2

--- a/solution.py
+++ b/solution.py
@@ -202,40 +202,18 @@
         c.wait()
 
 
-def middle_kernel(
-    nw, ns, reach,
-    row_map, halo_in, image, dots, norm, halo, residual, alpha_out, beta_out, norm_out,
-    dot_w, dot_s, norm_w, norm_s, sems_s, sems_r,
-):
-    rows = image.shape[0]
-    lanes = image.shape[2]
-    greet((("wide", nw), ("sixteen", ns)))
-    dot_w[0] = fold(dots[...])
-    dot_s[0] = all_sum(dot_w, "wide", nw, sems_s.at[0], sems_r.at[0])
-    alpha = norm[...] / all_sum(dot_s, "sixteen", ns, sems_s.at[1], sems_r.at[1])
-
-    def step(r, carry):
-        value = halo_in[reach + r] - alpha * image[row_map[r]]
-        residual[r] = value
-        return carry + jnp.sum(value * value, axis=0, keepdims=True)
-
-    squares = lax.fori_loop(0, rows, step, jnp.zeros((1, lanes), jnp.float32))
-    norm_w[0] = fold(squares)
-    norm_s[0] = all_sum(norm_w, "wide", nw, sems_s.at[2], sems_r.at[2])
-    norm_next = all_sum(norm_s, "sixteen", ns, sems_s.at[3], sems_r.at[3])
-    beta = norm_next / norm[...]
+def middle_kernel(ns, reach, row_map, halo_in, image, alpha, beta, halo, send_sem, recv_sem):
+    greet((("sixteen", ns),))
 
     def direct(r, carry):
-        halo[reach + r] = residual[r] + beta * halo_in[reach + r]
+        before = halo_in[reach + r]
+        halo[reach + r] = (before - alpha[...] * image[row_map[r]]) + beta[...] * before
         return carry
 
-    lax.fori_loop(0, rows, direct, 0)
-    copies = halo_copies(halo, rows, reach, ns, sems_s.at[4], sems_r.at[4])
+    lax.fori_loop(0, image.shape[0], direct, 0)
+    copies = halo_copies(halo, image.shape[0], reach, ns, send_sem, recv_sem)
     for c in copies:
         c.start()
-    alpha_out[...] = alpha
-    beta_out[...] = beta
-    norm_out[...] = norm_next
     for c in copies:
         c.wait()
 
@@ -271,7 +249,8 @@
         own = own_of(pair, at)
         value = NUGGET_TERM * own + jnp.where(halves(even, fields), even, odd)
         store(pair, at, value)
-        dots[...] += jnp.sum(own * value, axis=0, keepdims=True)
+        dots[0:1] += jnp.sum(own * value, axis=0, keepdims=True)
+        dots[1:2] += jnp.sum(value * value, axis=0, keepdims=True)
 
 
 def shifted(staged, received, n, send_sem, recv_sem):
@@ -300,13 +279,43 @@
     lax.fori_loop(0, slots, one, 0)
 
 
+def keep(staged_image, local_image, slot, pairs, pair, at, value):
+    if staged_image.shape[0] == BLOCKS_DEV:
+        staged_image[slot, pair, pl.ds(at, GROUP), :] = value
+    else:
+        local_image[slot * pairs + pair, pl.ds(at, GROUP), :] = value
+
+
+def slot_of(ns, g):
+    return lax.rem(g + 1, BLOCKS_DEV) if ns == BLOCKS_DEV else g
+
+
+def send_image(ns, g, images, staged_image, local_image, chosen):
+    if ns == BLOCKS_DEV:
+        for k in range(ns):
+
+            @pl.when(g == (k - 1) % ns)
+            def _(k=k):
+                images[k].start()
+
+    else:
+
+        @pl.when(g == BLOCKS_DEV - 1)
+        def _():
+            stage(staged_image, local_image, 0, chosen)
+            for c in images:
+                c.start()
+
+
 def first_image_kernel(
-    ns, starts, span, reach, fields, strip_rows,
-    offs, step_block, chosen, halo, others, centre,
-    tiles, image, dots, received,
-    windows, staged, send_sem, recv_sem,
+    nw, ns, starts, span, reach, fields, strip_rows,
+    offs, step_block, chosen, halo, others, centre, norm,
+    tiles, image, alpha, beta, norm_next, received, received_image,
+    windows, dots, staged, staged_image, local_image, dot_w, dot_s,
+    send_sem, recv_sem, send_image_sem, recv_image_sem, sems_s, sems_r,
 ):
     g = pl.program_id(0)
+    slot = slot_of(ns, g)
     pairs = strip_rows // 2
     spread = 2.0 * strip_rows
     cutoff = 6.0 * strip_rows
@@ -316,7 +325,7 @@
     @pl.when(g == 0)
     def _():
         stage(staged, halo, reach, chosen)
-        greet((("sixteen", ns),))
+        greet((("wide", nw), ("sixteen", ns)))
         for c in shifted(staged, received, ns, send_sem, recv_sem):
             c.start()
         build_windows(halo, windows, starts, span, fields, strip_rows)
@@ -351,6 +360,7 @@
 
         def store(pair, at, value):
             image[pair, pl.ds(at, GROUP), :] = value
+            keep(staged_image, local_image, slot, pairs, pair, at, value)
 
         def own_of(pair, at):
             return halo[reach + block * pairs + pair, pl.ds(at, GROUP), :]
@@ -359,38 +369,46 @@
         return carry
 
     lax.fori_loop(0, len(starts), one, 0)
+    images = shifted(staged_image, received_image, ns, send_image_sem, recv_image_sem)
+    send_image(ns, g, images, staged_image, local_image, chosen)
 
     @pl.when(g == pl.num_programs(0) - 1)
     def _():
+        dot_w[0] = fold(dots[...])
+        dot_s[0] = all_sum(dot_w, "wide", nw, sems_s.at[0], sems_r.at[0])
+        total = all_sum(dot_s, "sixteen", ns, sems_s.at[1], sems_r.at[1])
+        step = norm[...] / total[0:1]
+        after = (norm[...] - 2.0 * step * total[0:1]) + step * step * total[1:2]
+        alpha[...] = step
+        beta[...] = after / norm[...]
+        norm_next[...] = after
         for c in shifted(staged, received, ns, send_sem, recv_sem):
             c.wait()
+        for c in images:
+            c.wait()
 
 
 def second_image_kernel(
     nw, ns, starts, span, reach, fields, strip_rows,
-    offs, step_block, chosen, halo, residual, norm, tiles,
-    alpha, received_residual, received_image,
-    windows, dots, staged, staged_image, local_image, dot_w, dot_s,
-    send_sem, recv_sem, send_image, recv_image, sems_s, sems_r,
+    offs, step_block, chosen, halo, norm, tiles,
+    alpha, received_image,
+    windows, dots, staged_image, local_image, dot_w, dot_s,
+    send_image_sem, recv_image_sem, sems_s, sems_r,
 ):
     g = pl.program_id(0)
     last = pl.num_programs(0) - 1
     pairs = strip_rows // 2
     wide = strip_rows * span
     rows = strip_rows * GROUP
-    by_owner = ns == BLOCKS_DEV
+    slot = slot_of(ns, g)
 
     @pl.when(g == 0)
     def _():
-        stage(staged, residual, 0, chosen)
         greet((("wide", nw), ("sixteen", ns)))
-        for c in shifted(staged, received_residual, ns, send_sem, recv_sem):
-            c.start()
         build_windows(halo, windows, starts, span, fields, strip_rows)
         dots[...] = jnp.zeros_like(dots)
 
     block = step_block[g]
-    slot = lax.rem(g + 1, BLOCKS_DEV) if by_owner else g
 
     def one(i, carry):
         acc = jnp.zeros((2 * rows, 2 * fields), jnp.float32)
@@ -403,10 +421,7 @@
             )
 
         def store(pair, at, value):
-            if by_owner:
-                staged_image[slot, pair, pl.ds(at, GROUP), :] = value
-            else:
-                local_image[slot * pairs + pair, pl.ds(at, GROUP), :] = value
+            keep(staged_image, local_image, slot, pairs, pair, at, value)
 
         def own_of(pair, at):
             return halo[reach + block * pairs + pair, pl.ds(at, GROUP), :]
@@ -415,38 +430,29 @@
         return carry
 
     lax.fori_loop(0, len(starts), one, 0)
-    images = shifted(staged_image, received_image, ns, send_image, recv_image)
-    if by_owner:
-        for k in range(ns):
-
-            @pl.when(g == (k - 1) % ns)
-            def _(k=k):
-                images[k].start()
+    images = shifted(staged_image, received_image, ns, send_image_sem, recv_image_sem)
+    send_image(ns, g, images, staged_image, local_image, chosen)
 
     @pl.when(g == last)
     def _():
-        if not by_owner:
-            stage(staged_image, local_image, 0, chosen)
-            for c in images:
-                c.start()
         dot_w[0] = fold(dots[...])
         dot_s[0] = all_sum(dot_w, "wide", nw, sems_s.at[0], sems_r.at[0])
-        alpha[...] = norm[...] / all_sum(dot_s, "sixteen", ns, sems_s.at[1], sems_r.at[1])
-        for c in shifted(staged, received_residual, ns, send_sem, recv_sem):
-            c.wait()
+        total = all_sum(dot_s, "sixteen", ns, sems_s.at[1], sems_r.at[1])
+        alpha[...] = norm[...] / total[0:1]
         for c in images:
             c.wait()
 
 
-def final_kernel(fields, strip_rows, came, start, residual, image, alpha0, alpha1, beta, out, rest):
+def final_kernel(fields, strip_rows, came, start, middle, image, alpha0, alpha1, beta, out, rest):
     pairs, cols = start.shape[1:3]
     lead = alpha0[...] + alpha1[...] * beta[...]
     step = alpha1[...]
     for j in range(BLOCKS_DEV):
         k = came[j]
         for pair in range(pairs):
-            value = residual[k, pair]
-            first = (lead * start[k, pair] + step * value).T
+            first = start[k, pair]
+            value = first - alpha0[...] * middle[k, pair]
+            first = (lead * first + step * value).T
             second = (value - step * image[k, pair]).T
             for parity in range(2):
                 at = (2 * pair + parity) * cols
@@ -553,10 +559,16 @@
     moved_shape = shape((ns, pairs, col_dev, lanes), f32)
     staging = pltpu.VMEM(moved_shape.shape, f32)
 
-    tiles, image, dots, start = pl.pallas_call(
-        functools.partial(first_image_kernel, ns, *static),
+    sum_scratch = [
+        pltpu.VMEM((2, lanes), f32),
+        pltpu.VMEM((nw, 2, lanes), f32),
+        pltpu.VMEM((ns, 2, lanes), f32),
+    ]
+    local = pltpu.VMEM((8, 128) if ns == BLOCKS_DEV else (rows, col_dev, lanes), f32)
+    tiles, image, alpha0, beta, norm1, start, first_image = pl.pallas_call(
+        functools.partial(first_image_kernel, nw, ns, *static),
         grid=(BLOCKS_DEV,),
-        out_shape=(tile_shape, image_shape, dots_shape, moved_shape),
+        out_shape=(tile_shape, image_shape) + (dots_shape,) * 3 + (moved_shape,) * 2,
         in_specs=[
             SMEM,
             SMEM,
@@ -564,58 +576,36 @@
             whole_halo,
             pl.BlockSpec((blocks_halo, groups, 2, wide), lambda g: (0, 0, 0, 0)),
             pl.BlockSpec((BLOCKS_DEV, groups, strip_rows * GROUP, 2), lambda g: (0, 0, 0, 0)),
+            dots_spec,
         ],
-        out_specs=(tile_spec, image_spec, dots_spec, anywhere),
-        scratch_shapes=[window_scratch, staging] + [pltpu.SemaphoreType.DMA((ns,))] * 2,
+        out_specs=(tile_spec, image_spec) + (dots_spec,) * 3 + (anywhere,) * 2,
+        scratch_shapes=[window_scratch, sum_scratch[0], staging, staging, local]
+        + sum_scratch[1:]
+        + [pltpu.SemaphoreType.DMA((ns,))] * 4
+        + [pltpu.SemaphoreType.DMA((2, most))] * 2,
         compiler_params=pltpu.CompilerParams(collective_id=3, has_side_effects=True),
-    )(offs, step_block, chosen, halo, others, centre)
-
-    def mid(name_id, kernel, args, out_shape, phases, extra):
-        return pl.pallas_call(
-            kernel,
-            out_shape=out_shape,
-            in_specs=[SMEM] + [VMEM] * (len(args) - 1),
-            out_specs=(VMEM,) * len(out_shape),
-            scratch_shapes=[pltpu.VMEM((n, 1, lanes), f32) for _ in range(extra) for n in (nw, ns)]
-            + [pltpu.SemaphoreType.DMA((phases, most))] * 2,
-            compiler_params=pltpu.CompilerParams(collective_id=name_id, has_side_effects=True),
-        )(*args)
-
-    halo1, residual, alpha0, beta, norm1 = mid(
-        1,
-        functools.partial(middle_kernel, nw, ns, reach),
-        (row_map, halo, image, dots, norm),
-        (shape(halo.shape, f32), image_shape, dots_shape, dots_shape, dots_shape),
-        5,
-        2,
-    )
-    alpha1, mid_residual, last_image = pl.pallas_call(
+    )(offs, step_block, chosen, halo, others, centre, norm)
+
+    halo1 = pl.pallas_call(
+        functools.partial(middle_kernel, ns, reach),
+        out_shape=shape(halo.shape, f32),
+        in_specs=[SMEM] + [VMEM] * 4,
+        out_specs=VMEM,
+        scratch_shapes=[pltpu.SemaphoreType.DMA((2,))] * 2,
+        compiler_params=pltpu.CompilerParams(collective_id=1, has_side_effects=True),
+    )(row_map, halo, image, alpha0, beta)
+    alpha1, last_image = pl.pallas_call(
         functools.partial(second_image_kernel, nw, ns, *static),
         grid=(BLOCKS_DEV,),
-        out_shape=(dots_shape, moved_shape, moved_shape),
-        in_specs=[
-            SMEM,
-            SMEM,
-            SMEM,
-            whole_halo,
-            pl.BlockSpec((rows, col_dev, lanes), lambda g: (0, 0, 0)),
-            dots_spec,
-            tile_spec,
-        ],
-        out_specs=(dots_spec, anywhere, anywhere),
-        scratch_shapes=[
-            window_scratch,
-            pltpu.VMEM((1, lanes), f32),
-            staging,
-            staging,
-            pltpu.VMEM((8, 128) if ns == BLOCKS_DEV else (rows, col_dev, lanes), f32),
-            pltpu.VMEM((nw, 1, lanes), f32),
-            pltpu.VMEM((ns, 1, lanes), f32),
-        ]
-        + [pltpu.SemaphoreType.DMA((ns,))] * 4
+        out_shape=(dots_shape, moved_shape),
+        in_specs=[SMEM, SMEM, SMEM, whole_halo, dots_spec, tile_spec],
+        out_specs=(dots_spec, anywhere),
+        scratch_shapes=[window_scratch, sum_scratch[0], staging, local]
+        + sum_scratch[1:]
+        + [pltpu.SemaphoreType.DMA((ns,))] * 2
         + [pltpu.SemaphoreType.DMA((2, most))] * 2,
         compiler_params=pltpu.CompilerParams(collective_id=2, has_side_effects=True),
-    )(offs, step_block, chosen, halo1, residual, norm1, tiles)
+    )(offs, step_block, chosen, halo1, norm1, tiles)
 
     out_shape = shape((fields, BLOCKS_DEV, BLOCK), f32)
     solution_now, residual_now = pl.pallas_call(
@@ -623,7 +613,7 @@
         out_shape=(out_shape, out_shape),
         in_specs=[SMEM] + [VMEM] * 6,
         out_specs=(VMEM, VMEM),
-    )(came, start, mid_residual, last_image, alpha0, alpha1, beta)
+    )(came, start, first_image, last_image, alpha0, alpha1, beta)
     return solution_now[None, None], residual_now[None, None]
 
 

time: 237 us -> 217 us (0.916)
  Pallas kernels: 217 us -> 199 us
    pallas_call x1, Pallas kernels: 54.4 us -> 41 us  [on_device(): pl.pallas_call(functools.partial(second_image_kernel, nw, ns, *static), g...]
    pallas_call x2, Pallas kernels: 102 us -> 96.5 us  [the longest x1 65.9 us: on_device(): pl.pallas_call(functools.partial(first_image_kernel, nw, ns, *static), gr...]
where the time goes in v3:
time: 217 us
  Pallas kernels  199 us (92%)
  local copies, waits for them, and re-layouts  11.8 us (5%)
  other arithmetic  5.72 us (3%)
    pallas_call x1, Pallas kernels, on_device(): pl.pallas_call(functools.partial(first_image_kernel, nw, ns, *static), gr...  65.9 us
    pallas_call x1, Pallas kernels, on_device(): pl.pallas_call(functools.partial(polish_kernel, nw, ns, fields, reach), o...  55.5 us
    pallas_call x1, Pallas kernels, on_device(): pl.pallas_call(functools.partial(second_image_kernel, nw, ns, *static), g...  41 us
    pallas_call x1, Pallas kernels, on_device(): pl.pallas_call(functools.partial(middle_kernel, ns, reach), out_shape=sha...  30.6 us
    pallas_call x1, Pallas kernels, on_device(): pl.pallas_call(functools.partial(final_kernel, fields, strip_rows), out_s...  5.56 us

profile of v3, /device:TPU:0, one launch (start us, length us, event | category | flops | bytes accessed | tf_op | source)
XLA Modules:
  0.0 216.9 jit_solution(9785071971276634977)
XLA Ops:
  0.6 0.7 fusion.8
  1.3 0.2 reduce_window_sum.11
  1.5 0.2 multiply_reduce_fusion
  1.7 0.6 and_select_fusion
  2.3 0.9 add_reduce_fusion
  3.2 0.6 pad_add_fusion.offs
  3.8 0.7 dynamic-slice_bitcast_fusion
  4.5 0.2 select_reduce_fusion.1.chosen
  4.7 0.0 copy-start.2
  4.7 0.1 slice.38
  4.8 0.7 pad_add_fusion.1.step_block
  5.4 0.0 copy-start.1
  5.4 1.8 copy.41
  7.3 1.3 copy.42.obs
  8.6 0.0 copy-done.2
  8.6 0.0 copy-done.1
  8.6 0.0 copy-start.4
  8.6 0.0 copy-start
  8.6 0.1 broadcast_in_dim.11
  8.7 1.3 copy.43.weight
  10.0 0.0 copy-done.4
  10.0 0.6 maximum_bitcast_fusion.1.scale
  10.7 0.0 copy-done
  10.7 0.1 broadcast_add_fusion
  10.8 0.6 pad_maximum_fusion.place
  11.4 55.5 %shard_map.77 = (f32[32,128,128]{2,1,0:T(8,128)}, f32[64,2,128]{2,1,0:T(2,128)}, f32[1,128]{1,0:T(1,128)}) custom-call(f32[16,128,128]{2,1,0:T(8,128)} %copy.42.obs, f32[16,128,128]{2,1,0:T(8,128)} %copy.43.weight, f32[1,128]{1,0:T(1,128)} %maximum_bitcast_fusion.1.scale, f32[32,2,128]{2,1,0:T(2,128)} %pad_maximum_fusion.place), custom_call_target="tpu_custom_call" | custom-call | tf_op jit(solution)/shard_map/pallas_call | solution.py:489
  67.0 1.5 fusion.13
  68.7 1.1 reshape.204.others
  69.8 0.1 squeeze.20
  69.9 0.1 squeeze.19
  70.0 0.1 bitcast_add_fusion
  70.2 2.9 %copy.52 = f32[8,8,4,16,2]{4,3,2,1,0:T(8,128)} copy(f32[8,8,4,16,2]{3,1,4,2,0:T(8,128)S(1)} %maximum_bitcast_fusion) | data formatting | bytes 65536 | tf_op jit(solution)/shard_map/transpose | solution.py:527
  73.1 0.0 copy-start.3
  73.1 65.9 %shard_map.78 = (bf16[8,8,128,1792]{3,2,1,0:T(8,128)(2,1)}, f32[16,128,128]{2,1,0:T(8,128)}, f32[1,128]{1,0:T(1,128)}, f32[1,128]{1,0:T(1,128)}, f32[1,128]{1,0:...) custom-call(s32[7]{0:T(128)} %pad_add_fusion.offs, s32[8]{0:T(128)} %pad_add_fusion.1.step_block, ...), custom_call_target="tpu_custom_call" | custom-call | tf_op jit(solution)/shard_map/pallas_call | solution.py:568
  139.0 0.0 copy-done.3
  139.0 0.1 select_reduce_fusion
  139.1 0.1 iota_add_fusion
  139.2 0.6 add.180.row_map
  139.8 30.6 %shard_map.79.halo = f32[32,128,128]{2,1,0:T(8,128)} custom-call(s32[16]{0:T(128)} %add.180.row_map, f32[32,128,128]{2,1,0:T(8,128)} %get-tuple-element.16.halo.halo_in, f32[16,128,128]{2,1,0:T(8,128)} %get-tuple-element.21.image, f32[1,128]{1,0:T(1,128)} %get-tuple-element.22.alpha.alpha0, f32[1,128]{1,0:T(1,128)} %get-tuple-element.23.beta), custom_call_target="tpu_custom_call" | custom-call | tf_op jit(solution)/shard_map/pallas_call | solution.py:589
  170.3 41.0 %shard_map.80 = (f32[1,128]{1,0:T(1,128)}, f32[8,2,128,128]{3,2,1,0:T(8,128)}) custom-call(s32[7]{0:T(128)} %pad_add_fusion.offs, s32[8]{0:T(128)} %pad_add_fusion.1.step_block, s32[8]{0:T(128)} %copy-done.2, f32[32,128,128]{2,1,0:T(8,128)} %shard_map.79.halo, f32[1,128]{1,0:T(1,128)} %get-tuple-element.24.norm, ...), custom_call_target="tpu_custom_call" | custom-call | tf_op jit(solution)/shard_map/pallas_call | solution.py:597
  211.4 5.6 %shard_map.81 = (f32[64,8,512]{2,1,0:T(8,128)}, f32[64,8,512]{2,1,0:T(8,128)}) custom-call(s32[8]{0:T(128)} %get-tuple-element.39.came, f32[8,2,128,128]{3,2,1,0:T(8,128)} %get-tuple-element.19.start, f32[8,2,128,128]{3,2,1,0:T(8,128)} %get-tuple-element.20.middle, f32[8,2,128,128]{3,2,1,0:T(8,128)} %get-tuple-element.26.image, ...), custom_call_target="tpu_custom_call" | custom-call | tf_op jit(solution)/shard_map/pallas_call | solution.py:611
  (18 shorter events, 0.3 us)
Async XLA Ops:
  4.7 3.9 %copy-start.2 = (s32[8]{0:T(128)}, s32[8]{0:T(128)S(1)}, u32[]{:S(2)}) copy-start(s32[8]{0:T(128)S(1)} %select_reduce_fusion.1.chosen) | copy-start | bytes 100
  5.4 3.2 %copy-start.1 = (s32[32,128]{1,0:T(8,128)S(1)}, s32[32,128]{1,0:T(8,128)}, u32[]{:S(2)}) copy-start(s32[32,128]{1,0:T(8,128)} %param.8) | copy-start | bytes 49156
  8.6 1.4 copy-start.4
  8.6 2.1 copy-start
  73.1 65.9 %copy-start.3 = (s32[8]{0:T(128)S(1)}, s32[8]{0:T(128)}, u32[]{:S(2)}) copy-start(s32[8]{0:T(128)} %pad_add_fusion.1.step_block) | copy-start | bytes 100

commit v4 on v3

--- a/solution.py
+++ b/solution.py
@@ -110,10 +110,26 @@
     ]
 
 
+def edge_copies(source, target, reach, n, send_sem, recv_sem):
+    me = lax.axis_index("sixteen")
+    rows = source.shape[0]
+    return [
+        pltpu.make_async_remote_copy(
+            src_ref=source.at[pl.ds(first, reach)],
+            dst_ref=target.at[pl.ds(side * reach, reach)],
+            send_sem=send_sem.at[side],
+            recv_sem=recv_sem.at[side],
+            device_id={"sixteen": lax.rem(me + shift, n)},
+            device_id_type=MESH,
+        )
+        for side, first, shift in ((0, rows - reach, 1), (1, 0, n - 1))
+    ]
+
+
 def polish_kernel(
     nw, ns, fields, reach,
     obs, weight, scale, place, halo, place_halo, norm,
-    row_eff, row_cnt, col_eff, col_cnt,
+    row_eff, row_cnt, col_eff, col_cnt, obs_edge, row_edge,
     row_buf0, row_buf1, col_buf0, col_buf1, norm_w, norm_s,
     sems_s, sems_r,
 ):
@@ -126,7 +142,9 @@
     place_copies = halo_copies(
         place_halo, place_rows, place_reach, ns, sems_s.at[6], sems_r.at[6]
     )
-    for c in place_copies:
+    obs_copies = edge_copies(obs, obs_edge, reach, ns, sems_s.at[7], sems_r.at[7])
+    row_copies = edge_copies(row_eff, row_edge, reach, ns, sems_s.at[8], sems_r.at[8])
+    for c in place_copies + obs_copies:
         c.start()
     edge = HUBER_EDGE
     diagonal = lax.broadcasted_iota(jnp.int32, (cols, lanes), 0) == lax.broadcasted_iota(
@@ -154,6 +172,9 @@
         if sweep == 0:
             row_cnt[...] = jnp.maximum(total[rows:], 1.0)
         row_eff[...] = row_eff[...] + scale[...] * total[:rows] / row_cnt[...]
+        if sweep == SWEEPS - 1:
+            for c in row_copies:
+                c.start()
 
         def col_step(r, carry):
             return carry + clipped(r)
@@ -192,14 +213,30 @@
         return carry + jnp.sum(value * value, axis=0, keepdims=True)
 
     squares = lax.fori_loop(0, rows, rest, jnp.zeros((1, lanes), jnp.float32))
-    copies = halo_copies(halo, rows, reach, ns, sems_s.at[7], sems_r.at[7])
-    for c in copies:
-        c.start()
     norm_w[0] = fold(squares)
     norm_s[0] = all_sum(norm_w, "wide", nw, sems_s.at[4], sems_r.at[4])
     norm[...] = all_sum(norm_s, "sixteen", ns, sems_s.at[5], sems_r.at[5])
-    for c in copies + place_copies:
+    for c in place_copies + row_copies + obs_copies:
         c.wait()
+
+    def across(row):
+        spread = jnp.where(diagonal, jnp.broadcast_to(row, (cols, lanes)), 0.0)
+        return jnp.broadcast_to(jnp.sum(spread, axis=1, keepdims=True), (cols, lanes))
+
+    def beside(first):
+        def one(q, carry):
+            t = first + q
+            even = across(place_halo[2 * t, 2:3])
+            odd = across(place_halo[2 * t + 1, 2:3])
+            seen = jnp.where(halves(even, fields), even, odd)
+            at = q if first == 0 else reach + q
+            halo[t] = seen * (obs_edge[at] - row_edge[pl.ds(at, 1)] - col_eff[...])
+            return carry
+
+        lax.fori_loop(0, reach, one, 0)
+
+    beside(0)
+    beside(reach + rows)
 
 
 def middle_kernel(ns, reach, row_map, halo_in, image, alpha, beta, halo, send_sem, recv_sem):
@@ -483,14 +520,15 @@
     row_place = (my_place * row_dev + jnp.arange(row_dev, dtype=jnp.int32)).astype(f32)
     col_place = (group_place * col_dev + jnp.arange(col_dev, dtype=jnp.int32)).astype(f32)
     place = jnp.stack(
-        [row_place[:, None] + jitter[0], col_place[None, :] + jitter[1]], axis=1
+        [row_place[:, None] + jitter[0], col_place[None, :] + jitter[1], observed.astype(f32)],
+        axis=1,
     )
     most = max(nw, ns)
     halo, place_halo, norm = pl.pallas_call(
         functools.partial(polish_kernel, nw, ns, fields, reach),
         out_shape=(
             shape((rows + 2 * reach, col_dev, lanes), f32),
-            shape((row_dev + 4 * reach, 2, col_dev), f32),
+            shape((row_dev + 4 * reach, 3, col_dev), f32),
             shape((1, lanes), f32),
         ),
         in_specs=[VMEM] * 4,
@@ -500,14 +538,16 @@
             pltpu.VMEM((rows, lanes), f32),
             pltpu.VMEM((col_dev, lanes), f32),
             pltpu.VMEM((col_dev, lanes), f32),
+            pltpu.VMEM((2 * reach, col_dev, lanes), f32),
+            pltpu.VMEM((2 * reach, lanes), f32),
             pltpu.VMEM((nw, 2 * rows, lanes), f32),
             pltpu.VMEM((nw, rows, lanes), f32),
             pltpu.VMEM((ns, col_dev // 2 + 8, lanes), f32),
             pltpu.VMEM((ns, col_dev // 2, lanes), f32),
             pltpu.VMEM((nw, 1, lanes), f32),
             pltpu.VMEM((ns, 1, lanes), f32),
-            pltpu.SemaphoreType.DMA((8, most)),
-            pltpu.SemaphoreType.DMA((8, most)),
+            pltpu.SemaphoreType.DMA((9, most)),
+            pltpu.SemaphoreType.DMA((9, most)),
         ],
         compiler_params=pltpu.CompilerParams(collective_id=0, has_side_effects=True),
     )(obs, weight, scale, place)
@@ -520,10 +560,10 @@
     groups = len(starts)
     wide = strip_rows * span
     blocks_halo = BLOCKS_DEV + 2 * REACH
-    by_block = place_halo.reshape(blocks_halo, strip_rows, 2, col_dev)
+    by_block = place_halo[:, :2].reshape(blocks_halo, strip_rows, 2, col_dev)
     others = jnp.stack([by_block[..., s : s + span] for s in starts], axis=1)
     others = others.transpose(0, 1, 3, 2, 4).reshape(blocks_halo, groups, 2, wide)
-    centre = place.reshape(BLOCKS_DEV, strip_rows, 2, groups, GROUP)
+    centre = place[:, :2].reshape(BLOCKS_DEV, strip_rows, 2, groups, GROUP)
     centre = centre.transpose(0, 3, 1, 4, 2).reshape(BLOCKS_DEV, groups, strip_rows * GROUP, 2)
     listed = (neighbours[0, 0] + total_strips // 2) % total_strips - total_strips // 2
     offs = jnp.concatenate([jnp.zeros((1,), jnp.int32), listed])

time: 217 us -> 217 us (level)
    pallas_call x1, Pallas kernels: 55.5 us -> 58.7 us  [on_device(): pl.pallas_call(functools.partial(polish_kernel, nw, ns, fields, reach), o...]
    pallas_call x1, Pallas kernels: 30.6 us -> 28.2 us  [on_device(): pl.pallas_call(functools.partial(middle_kernel, ns, reach), out_shape=sha...]
where the time goes in v4:
time: 217 us
  Pallas kernels  199 us (92%)
  local copies, waits for them, and re-layouts  11.7 us (5%)
  other arithmetic  5.76 us (3%)
    pallas_call x1, Pallas kernels, on_device(): pl.pallas_call(functools.partial(first_image_kernel, nw, ns, *static), gr...  64.9 us
    pallas_call x1, Pallas kernels, on_device(): pl.pallas_call(functools.partial(polish_kernel, nw, ns, fields, reach), o...  58.7 us
    pallas_call x1, Pallas kernels, on_device(): pl.pallas_call(functools.partial(second_image_kernel, nw, ns, *static), g...  41.3 us
    pallas_call x1, Pallas kernels, on_device(): pl.pallas_call(functools.partial(middle_kernel, ns, reach), out_shape=sha...  28.2 us
    pallas_call x1, Pallas kernels, on_device(): pl.pallas_call(functools.partial(final_kernel, fields, strip_rows), out_s...  5.56 us

profile of v4, /device:TPU:0, one launch (start us, length us, event | category | flops | bytes accessed | tf_op | source)
XLA Modules:
  0.0 216.9 jit_solution(8069285322258810297)
XLA Ops:
  0.6 0.7 fusion.8
  1.3 0.2 reduce_window_sum.11
  1.5 0.2 multiply_reduce_fusion
  1.7 0.6 and_select_fusion
  2.3 0.9 add_reduce_fusion
  3.2 0.6 pad_add_fusion.offs
  3.8 0.7 dynamic-slice_bitcast_fusion
  4.5 0.2 select_reduce_fusion.1.chosen
  4.7 0.0 copy-start.2
  4.7 0.1 slice.43
  4.8 0.7 pad_add_fusion.1.step_block
  5.4 0.0 copy-start.1
  5.4 1.8 copy.41
  7.3 1.3 copy.42.obs
  8.6 0.0 copy-done.2
  8.6 0.0 copy-done.1
  8.6 0.0 copy-start.4
  8.6 0.0 copy-start
  8.6 0.1 broadcast_in_dim.11
  8.7 1.3 copy.43.weight
  10.0 0.0 copy-done.4
  10.0 0.6 maximum_bitcast_fusion.1.scale
  10.7 0.0 copy-done
  10.7 0.1 broadcast_add_fusion
  10.8 0.7 pad_maximum_fusion.place
  11.5 58.7 %shard_map.77 = (f32[32,128,128]{2,1,0:T(8,128)}, f32[64,3,128]{2,1,0:T(4,128)}, f32[1,128]{1,0:T(1,128)}) custom-call(f32[16,128,128]{2,1,0:T(8,128)} %copy.42.obs, f32[16,128,128]{2,1,0:T(8,128)} %copy.43.weight, f32[1,128]{1,0:T(1,128)} %maximum_bitcast_fusion.1.scale, f32[32,3,128]{2,1,0:T(4,128)} %pad_maximum_fusion.place), custom_call_target="tpu_custom_call" | custom-call | tf_op jit(solution)/shard_map/pallas_call | solution.py:527
  70.1 0.9 slice.47
  71.1 0.4 fusion.13
  71.7 1.1 reshape.198.others
  72.8 0.1 squeeze.20
  72.9 0.1 squeeze.19
  73.1 0.1 bitcast_add_fusion
  73.2 2.9 %copy.52 = f32[8,8,4,16,2]{4,3,2,1,0:T(8,128)} copy(f32[8,8,4,16,2]{3,1,4,2,0:T(8,128)S(1)} %maximum_bitcast_fusion) | data formatting | bytes 65536 | tf_op jit(solution)/shard_map/transpose | solution.py:567
  76.1 0.0 copy-start.3
  76.1 64.9 %shard_map.78 = (bf16[8,8,128,1792]{3,2,1,0:T(8,128)(2,1)}, f32[16,128,128]{2,1,0:T(8,128)}, f32[1,128]{1,0:T(1,128)}, f32[1,128]{1,0:T(1,128)}, f32[1,128]{1,0:...) custom-call(s32[7]{0:T(128)} %pad_add_fusion.offs, s32[8]{0:T(128)} %pad_add_fusion.1.step_block, ...), custom_call_target="tpu_custom_call" | custom-call | tf_op jit(solution)/shard_map/pallas_call | solution.py:608
  141.0 0.0 copy-done.3
  141.0 0.1 select_reduce_fusion
  141.1 0.1 iota_add_fusion
  141.2 0.6 add.176.row_map
  141.8 28.2 %shard_map.79.halo = f32[32,128,128]{2,1,0:T(8,128)} custom-call(s32[16]{0:T(128)} %add.176.row_map, f32[32,128,128]{2,1,0:T(8,128)} %get-tuple-element.16.halo.halo_in, f32[16,128,128]{2,1,0:T(8,128)} %get-tuple-element.21.image, f32[1,128]{1,0:T(1,128)} %get-tuple-element.22.alpha.alpha0, f32[1,128]{1,0:T(1,128)} %get-tuple-element.23.beta), custom_call_target="tpu_custom_call" | custom-call | tf_op jit(solution)/shard_map/pallas_call | solution.py:629
  170.0 41.3 %shard_map.80 = (f32[1,128]{1,0:T(1,128)}, f32[8,2,128,128]{3,2,1,0:T(8,128)}) custom-call(s32[7]{0:T(128)} %pad_add_fusion.offs, s32[8]{0:T(128)} %pad_add_fusion.1.step_block, s32[8]{0:T(128)} %copy-done.2, f32[32,128,128]{2,1,0:T(8,128)} %shard_map.79.halo, f32[1,128]{1,0:T(1,128)} %get-tuple-element.24.norm, ...), custom_call_target="tpu_custom_call" | custom-call | tf_op jit(solution)/shard_map/pallas_call | solution.py:637
  211.3 5.6 %shard_map.81 = (f32[64,8,512]{2,1,0:T(8,128)}, f32[64,8,512]{2,1,0:T(8,128)}) custom-call(s32[8]{0:T(128)} %get-tuple-element.39.came, f32[8,2,128,128]{3,2,1,0:T(8,128)} %get-tuple-element.19.start, f32[8,2,128,128]{3,2,1,0:T(8,128)} %get-tuple-element.20.middle, f32[8,2,128,128]{3,2,1,0:T(8,128)} %get-tuple-element.26.image, ...), custom_call_target="tpu_custom_call" | custom-call | tf_op jit(solution)/shard_map/pallas_call | solution.py:651
  (18 shorter events, 0.3 us)
Async XLA Ops:
  4.7 3.9 %copy-start.2 = (s32[8]{0:T(128)}, s32[8]{0:T(128)S(1)}, u32[]{:S(2)}) copy-start(s32[8]{0:T(128)S(1)} %select_reduce_fusion.1.chosen) | copy-start | bytes 100
  5.4 3.2 %copy-start.1 = (s32[32,128]{1,0:T(8,128)S(1)}, s32[32,128]{1,0:T(8,128)}, u32[]{:S(2)}) copy-start(s32[32,128]{1,0:T(8,128)} %param.8) | copy-start | bytes 49156
  8.6 1.4 copy-start.4
  8.6 2.1 copy-start
  76.1 64.9 %copy-start.3 = (s32[8]{0:T(128)S(1)}, s32[8]{0:T(128)}, u32[]{:S(2)}) copy-start(s32[8]{0:T(128)} %pad_add_fusion.1.step_block) | copy-start | bytes 100

commit v5 on v4

--- a/solution.py
+++ b/solution.py
@@ -128,9 +128,9 @@
 
 def polish_kernel(
     nw, ns, fields, reach,
-    obs, weight, scale, place, halo, place_halo, norm,
+    obs, weight, scale, place, halo, place_halo,
     row_eff, row_cnt, col_eff, col_cnt, obs_edge, row_edge,
-    row_buf0, row_buf1, col_buf0, col_buf1, norm_w, norm_s,
+    row_buf0, row_buf1, col_buf0, col_buf1,
     sems_s, sems_r,
 ):
     rows, cols, lanes = obs.shape
@@ -210,12 +210,9 @@
     def rest(r, carry):
         value = weight[r] * (obs[r] - row_eff[pl.ds(r, 1)] - col_eff[...])
         halo[reach + r] = value
-        return carry + jnp.sum(value * value, axis=0, keepdims=True)
-
-    squares = lax.fori_loop(0, rows, rest, jnp.zeros((1, lanes), jnp.float32))
-    norm_w[0] = fold(squares)
-    norm_s[0] = all_sum(norm_w, "wide", nw, sems_s.at[4], sems_r.at[4])
-    norm[...] = all_sum(norm_s, "sixteen", ns, sems_s.at[5], sems_r.at[5])
+        return carry
+
+    lax.fori_loop(0, rows, rest, 0)
     for c in place_copies + row_copies + obs_copies:
         c.wait()
 
@@ -288,6 +285,7 @@
         store(pair, at, value)
         dots[0:1] += jnp.sum(own * value, axis=0, keepdims=True)
         dots[1:2] += jnp.sum(value * value, axis=0, keepdims=True)
+        dots[2:3] += jnp.sum(own * own, axis=0, keepdims=True)
 
 
 def shifted(staged, received, n, send_sem, recv_sem):
@@ -346,7 +344,7 @@
 
 def first_image_kernel(
     nw, ns, starts, span, reach, fields, strip_rows,
-    offs, step_block, chosen, halo, others, centre, norm,
+    offs, step_block, chosen, halo, others, centre,
     tiles, image, alpha, beta, norm_next, received, received_image,
     windows, dots, staged, staged_image, local_image, dot_w, dot_s,
     send_sem, recv_sem, send_image_sem, recv_image_sem, sems_s, sems_r,
@@ -414,10 +412,11 @@
         dot_w[0] = fold(dots[...])
         dot_s[0] = all_sum(dot_w, "wide", nw, sems_s.at[0], sems_r.at[0])
         total = all_sum(dot_s, "sixteen", ns, sems_s.at[1], sems_r.at[1])
-        step = norm[...] / total[0:1]
-        after = (norm[...] - 2.0 * step * total[0:1]) + step * step * total[1:2]
+        norm = total[2:3]
+        step = norm / total[0:1]
+        after = (norm - 2.0 * step * total[0:1]) + step * step * total[1:2]
         alpha[...] = step
-        beta[...] = after / norm[...]
+        beta[...] = after / norm
         norm_next[...] = after
         for c in shifted(staged, received, ns, send_sem, recv_sem):
             c.wait()
@@ -524,15 +523,14 @@
         axis=1,
     )
     most = max(nw, ns)
-    halo, place_halo, norm = pl.pallas_call(
+    halo, place_halo = pl.pallas_call(
         functools.partial(polish_kernel, nw, ns, fields, reach),
         out_shape=(
             shape((rows + 2 * reach, col_dev, lanes), f32),
             shape((row_dev + 4 * reach, 3, col_dev), f32),
-            shape((1, lanes), f32),
         ),
         in_specs=[VMEM] * 4,
-        out_specs=(VMEM,) * 3,
+        out_specs=(VMEM,) * 2,
         scratch_shapes=[
             pltpu.VMEM((rows, lanes), f32),
             pltpu.VMEM((rows, lanes), f32),
@@ -544,8 +542,6 @@
             pltpu.VMEM((nw, rows, lanes), f32),
             pltpu.VMEM((ns, col_dev // 2 + 8, lanes), f32),
             pltpu.VMEM((ns, col_dev // 2, lanes), f32),
-            pltpu.VMEM((nw, 1, lanes), f32),
-            pltpu.VMEM((ns, 1, lanes), f32),
             pltpu.SemaphoreType.DMA((9, most)),
             pltpu.SemaphoreType.DMA((9, most)),
         ],
@@ -600,9 +596,9 @@
     staging = pltpu.VMEM(moved_shape.shape, f32)
 
     sum_scratch = [
-        pltpu.VMEM((2, lanes), f32),
-        pltpu.VMEM((nw, 2, lanes), f32),
-        pltpu.VMEM((ns, 2, lanes), f32),
+        pltpu.VMEM((3, lanes), f32),
+        pltpu.VMEM((nw, 3, lanes), f32),
+        pltpu.VMEM((ns, 3, lanes), f32),
     ]
     local = pltpu.VMEM((8, 128) if ns == BLOCKS_DEV else (rows, col_dev, lanes), f32)
     tiles, image, alpha0, beta, norm1, start, first_image = pl.pallas_call(
@@ -616,7 +612,6 @@
             whole_halo,
             pl.BlockSpec((blocks_halo, groups, 2, wide), lambda g: (0, 0, 0, 0)),
             pl.BlockSpec((BLOCKS_DEV, groups, strip_rows * GROUP, 2), lambda g: (0, 0, 0, 0)),
-            dots_spec,
         ],
         out_specs=(tile_spec, image_spec) + (dots_spec,) * 3 + (anywhere,) * 2,
         scratch_shapes=[window_scratch, sum_scratch[0], staging, staging, local]
@@ -624,7 +619,7 @@
         + [pltpu.SemaphoreType.DMA((ns,))] * 4
         + [pltpu.SemaphoreType.DMA((2, most))] * 2,
         compiler_params=pltpu.CompilerParams(collective_id=3, has_side_effects=True),
-    )(offs, step_block, chosen, halo, others, centre, norm)
+    )(offs, step_block, chosen, halo, others, centre)
 
     halo1 = pl.pallas_call(
         functools.partial(middle_kernel, ns, reach),

time: 217 us -> 211 us (0.972)
  Pallas kernels: 199 us -> 193 us
    pallas_call x1, Pallas kernels: 58.7 us -> 50.3 us  [on_device(): pl.pallas_call(functools.partial(polish_kernel, nw, ns, fields, reach), o...]
where the time goes in v5:
time: 211 us
  Pallas kernels  193 us (91%)
  local copies, waits for them, and re-layouts  11.7 us (6%)
  other arithmetic  5.77 us (3%)
    pallas_call x1, Pallas kernels, on_device(): pl.pallas_call(functools.partial(first_image_kernel, nw, ns, *static), gr...  65 us
    pallas_call x1, Pallas kernels, on_device(): pl.pallas_call(functools.partial(polish_kernel, nw, ns, fields, reach), o...  50.3 us
    pallas_call x1, Pallas kernels, on_device(): pl.pallas_call(functools.partial(second_image_kernel, nw, ns, *static), g...  41.5 us
    pallas_call x1, Pallas kernels, on_device(): pl.pallas_call(functools.partial(middle_kernel, ns, reach), out_shape=sha...  30.3 us
    pallas_call x1, Pallas kernels, on_device(): pl.pallas_call(functools.partial(final_kernel, fields, strip_rows), out_s...  5.56 us

profile of v5, /device:TPU:0, one launch (start us, length us, event | category | flops | bytes accessed | tf_op | source)
XLA Modules:
  0.0 210.8 jit_solution(3946959562940326392)
XLA Ops:
  0.6 0.7 fusion.8
  1.3 0.2 reduce_window_sum.11
  1.5 0.2 multiply_reduce_fusion
  1.7 0.6 and_select_fusion
  2.3 0.9 add_reduce_fusion
  3.2 0.6 pad_add_fusion.offs
  3.8 0.7 dynamic-slice_bitcast_fusion
  4.5 0.2 select_reduce_fusion.1.chosen
  4.7 0.0 copy-start.2
  4.7 0.1 slice.43
  4.8 0.7 pad_add_fusion.1.step_block
  5.4 0.0 copy-start.1
  5.4 1.8 copy.41
  7.3 1.3 copy.42.obs
  8.6 0.0 copy-done.2
  8.6 0.0 copy-done.1
  8.6 0.0 copy-start.4
  8.6 0.0 copy-start
  8.6 0.1 broadcast_in_dim.11
  8.7 1.3 copy.43.weight
  10.0 0.0 copy-done.4
  10.0 0.7 maximum_bitcast_fusion.1.scale
  10.7 0.0 copy-done
  10.7 0.1 broadcast_add_fusion
  10.8 0.7 pad_maximum_fusion.place
  11.5 50.3 %shard_map.77 = (f32[32,128,128]{2,1,0:T(8,128)}, f32[64,3,128]{2,1,0:T(4,128)}) custom-call(f32[16,128,128]{2,1,0:T(8,128)} %copy.42.obs, f32[16,128,128]{2,1,0:T(8,128)} %copy.43.weight, f32[1,128]{1,0:T(1,128)} %maximum_bitcast_fusion.1.scale, f32[32,3,128]{2,1,0:T(4,128)} %pad_maximum_fusion.place), custom_call_target="tpu_custom_call" | custom-call | tf_op jit(solution)/shard_map/pallas_call | solution.py:526
  61.8 0.9 slice.47
  62.7 0.4 fusion.13
  63.4 1.1 reshape.198.others
  64.5 0.1 squeeze.20
  64.6 0.1 squeeze.19
  64.7 0.1 bitcast_add_fusion
  64.8 2.9 %copy.52 = f32[8,8,4,16,2]{4,3,2,1,0:T(8,128)} copy(f32[8,8,4,16,2]{3,1,4,2,0:T(8,128)S(1)} %maximum_bitcast_fusion) | data formatting | bytes 65536 | tf_op jit(solution)/shard_map/transpose | solution.py:563
  67.7 0.0 copy-start.3
  67.7 65.0 %shard_map.78 = (bf16[8,8,128,1792]{3,2,1,0:T(8,128)(2,1)}, f32[16,128,128]{2,1,0:T(8,128)}, f32[1,128]{1,0:T(1,128)}, f32[1,128]{1,0:T(1,128)}, f32[1,128]{1,0:...) custom-call(s32[7]{0:T(128)} %pad_add_fusion.offs, s32[8]{0:T(128)} %pad_add_fusion.1.step_block, ...), custom_call_target="tpu_custom_call" | custom-call | tf_op jit(solution)/shard_map/pallas_call | solution.py:604
  132.7 0.0 copy-done.3
  132.7 0.1 select_reduce_fusion
  132.8 0.1 iota_add_fusion
  132.9 0.6 add.176.row_map
  133.5 30.3 %shard_map.79.halo = f32[32,128,128]{2,1,0:T(8,128)} custom-call(s32[16]{0:T(128)} %add.176.row_map, f32[32,128,128]{2,1,0:T(8,128)} %get-tuple-element.15.halo.halo_in, f32[16,128,128]{2,1,0:T(8,128)} %get-tuple-element.19.image, f32[1,128]{1,0:T(1,128)} %get-tuple-element.20.alpha.alpha0, f32[1,128]{1,0:T(1,128)} %get-tuple-element.21.beta), custom_call_target="tpu_custom_call" | custom-call | tf_op jit(solution)/shard_map/pallas_call | solution.py:624
  163.8 41.5 %shard_map.80 = (f32[1,128]{1,0:T(1,128)}, f32[8,2,128,128]{3,2,1,0:T(8,128)}) custom-call(s32[7]{0:T(128)} %pad_add_fusion.offs, s32[8]{0:T(128)} %pad_add_fusion.1.step_block, s32[8]{0:T(128)} %copy-done.2, f32[32,128,128]{2,1,0:T(8,128)} %shard_map.79.halo, f32[1,128]{1,0:T(1,128)} %get-tuple-element.22.norm, ...), custom_call_target="tpu_custom_call" | custom-call | tf_op jit(solution)/shard_map/pallas_call | solution.py:632
  205.3 5.6 %shard_map.81 = (f32[64,8,512]{2,1,0:T(8,128)}, f32[64,8,512]{2,1,0:T(8,128)}) custom-call(s32[8]{0:T(128)} %get-tuple-element.37.came, f32[8,2,128,128]{3,2,1,0:T(8,128)} %get-tuple-element.17.start, f32[8,2,128,128]{3,2,1,0:T(8,128)} %get-tuple-element.18.middle, f32[8,2,128,128]{3,2,1,0:T(8,128)} %get-tuple-element.24.image, ...), custom_call_target="tpu_custom_call" | custom-call | tf_op jit(solution)/shard_map/pallas_call | solution.py:646
  (18 shorter events, 0.3 us)
Async XLA Ops:
  4.7 3.9 %copy-start.2 = (s32[8]{0:T(128)}, s32[8]{0:T(128)S(1)}, u32[]{:S(2)}) copy-start(s32[8]{0:T(128)S(1)} %select_reduce_fusion.1.chosen) | copy-start | bytes 100
  5.4 3.2 %copy-start.1 = (s32[32,128]{1,0:T(8,128)S(1)}, s32[32,128]{1,0:T(8,128)}, u32[]{:S(2)}) copy-start(s32[32,128]{1,0:T(8,128)} %param.8) | copy-start | bytes 49156
  8.6 1.4 copy-start.4
  8.6 2.1 copy-start
  67.7 65.0 %copy-start.3 = (s32[8]{0:T(128)S(1)}, s32[8]{0:T(128)}, u32[]{:S(2)}) copy-start(s32[8]{0:T(128)} %pad_add_fusion.1.step_block) | copy-start | bytes 100
